TPU v7x, 32 devices: a whole 2x2x4 slice. The times are simulated.
32 devices in a mesh: samp: 4 (over y, x), var: 8 (over z, core).
Axes of the slice: x: 2, y: 2, z: 4, core: 2. Of those that a mesh axis runs over, the one named last changes fastest.
Arguments:
- observed: bfloat16 [1024, 32768], P('samp', 'var'), may hold values from -6 to 6
- blocks: float32 [256, 2, 128, 128], P('var'), may hold values from -6 to 6
- diagonal: float32 [32768], P('var'), may hold values from 1 to 4
- pattern: int32 [256, 2], P('var'), may hold values from 0 to 255, as said below
Outputs:
- new_blocks: float32 [256, 2, 128, 128], P('var')
- new_diagonal: float32 [32768], P('var')
- objective: float32 [2], replicated
Inputs may be any that keep to these rules, and one draw needn't show every extreme that they name: pattern[c, 0] and pattern[c, 1] are two different row-block indices, one of them equal to c. For each index v of var, among its block columns c = v * 32 to v * 32 + 31, for every u, at most 4 of the entries that differ from c name row blocks in the range u * 32 to u * 32 + 31, and for some u exactly 4 do.
All inputs are finite; a program needn't handle non-finite values.
Results may differ from a plain program's by a relative error of at most 0.0049.
Values may be sent and summed in bfloat16 or wider, within the bound.
A program may use at most 128 MiB of HBM per device.

v0:
```python
import functools

import jax
import jax.numpy as jnp
from jax import lax
from jax.experimental import pallas as pl
from jax.experimental.pallas import tpu as pltpu
from jax.sharding import PartitionSpec as P

STEPS = 2


step_length = 0.5
penalty = 0.5
MESH = pl.DeviceIdType.MESH


def shrink(moved, level):
    return moved - jnp.clip(moved, -level, level)


def flip(index, offset, count):
    out, bit = 0, 1
    while bit < count:
        out = out + ((index // bit + offset // bit) % 2) * bit
        bit *= 2
    return out


def main_kernel(samp, var, near_idx, wanted, own_slot, want_ref, x_hbm, blk_hbm, dia_ref,
                fin_ref, tails_ref, obj_ref,
                x, blk, ask, ask_s, far, farz, cc_out, cc_in, cc_own, oo_out, oo_in, oo_own, oz, acc,
                load, ask_ss, ask_rs, ask_l, cc_s, cc_r, z_s, z_r, oo_s, oo_r, out_s, out_r,
                rel_s, rel_r, tail_s, tail_r, oz_s, oz_r):
    s = lax.axis_index("samp")
    v = lax.axis_index("var")
    rows, width = x.shape[1], x.shape[2]
    total_rows = rows * samp
    over_first = (((0,), (0,)), ((), ()))

    cols = x.shape[0]
    x_loads = [
        pltpu.make_async_copy(x_hbm.at[:, l * width:(l + 1) * width], x.at[l], load.at[l])
        for l in range(cols)
    ]
    for x_load in x_loads:
        x_load.start()
    blk_load = pltpu.make_async_copy(blk_hbm, blk, load.at[cols])
    blk_load.start()

    barrier = pltpu.get_barrier_semaphore()
    for i in range(1, var):
        pl.semaphore_signal(barrier, inc=1, device_id={"var": flip(v, i, var)}, device_id_type=MESH)
    for d in range(1, samp):
        pl.semaphore_signal(barrier, inc=1, device_id={"samp": flip(s, d, samp)}, device_id_type=MESH)
    pl.semaphore_wait(barrier, samp + var - 2)

    def remote(src, dst, send, recv, **where):
        return pltpu.make_async_remote_copy(
            src_ref=src, dst_ref=dst, send_sem=send, recv_sem=recv,
            device_id=where, device_id_type=MESH)

    def ask_copy(i):
        u = flip(v, i, var)
        return remote(want_ref.at[u], ask.at[v], ask_ss.at[i], ask_rs.at[i], var=u)

    def z_copy(i):
        u = flip(v, i, var)
        return remote(far.at[u], farz.at[v], z_s.at[i], z_r.at[i], var=u)

    def cc_copy(d, i):
        u, k = flip(v, i, var), flip(s, d, samp)
        return remote(cc_out.at[u, k], cc_in.at[u, s], cc_s.at[d, i], cc_r.at[d, i], samp=k)

    def oo_copy(d, i):
        u, k = flip(v, i, var), flip(s, d, samp)
        return remote(oo_out.at[u, k], oo_in.at[u, s], oo_s.at[d, i], oo_r.at[d, i], samp=k)

    def out_copy(d, i):
        u, k = flip(v, i, var), flip(s, d, samp)
        return remote(fin_ref.at[s, u], fin_ref.at[s, u], out_s.at[d, i], out_r.at[d, i], samp=k)

    def panel(index):
        return x[index]

    def near_panel(u, k):
        return panel(near_idx[u * samp + k])

    def gram(left, right):
        return lax.dot_general(left, right, over_first, preferred_element_type=jnp.float32)

    eye = lax.broadcasted_iota(jnp.int32, (width, width), 0) == lax.broadcasted_iota(
        jnp.int32, (width, width), 1)

    row_at = lax.broadcasted_iota(jnp.int32, (width, width), 0)
    col_at = lax.broadcasted_iota(jnp.int32, (width, width), 1)
    spare = (row_at == col_at + 1) | ((row_at == width - 1) & (col_at == 0))

    def rounded_symmetric(part):
        off = jnp.where(eye, part - part.astype(jnp.bfloat16).astype(jnp.float32), 0.0)
        row = jnp.sum(off, axis=0, keepdims=True)
        below = jnp.where(row_at == col_at + 1, row, part)
        corner = jnp.where((row_at == width - 1) & (col_at == 0), row[:, width - 1:], below)
        return corner.astype(jnp.bfloat16)

    def own_symmetric(part):
        return jnp.where(spare, 0.0, part)

    def restored(total):
        below = jnp.where(row_at == col_at + 1, total, 0.0)
        row = jnp.sum(below, axis=0, keepdims=True)
        last = total[width - 1:, :1]
        row = jnp.where(col_at[:1] == width - 1, last, row)
        return jnp.where(spare, total.T, total) + jnp.where(eye, row, 0.0)

    def start_cc(i):
        u = flip(v, i, var)
        for d in range(samp):
            k = flip(s, d, samp)
            c = near_panel(u, k)
            part = gram(c, c)
            if d == 0:
                cc_own[u] = own_symmetric(part)
            else:
                cc_out[u, k] = rounded_symmetric(part)
                cc_copy(d, i).start()

    def start_oo(i, far_panel):
        u = flip(v, i, var)
        for d in range(samp):
            k = flip(s, d, samp)
            o = far_panel(u, k)
            part = gram(o, jnp.concatenate([near_panel(u, k), o], axis=1))
            if d == 0:
                oo_own[u, :, :width] = part[:, :width]
                oo_own[u, :, width:] = own_symmetric(part[:, width:])
            else:
                oo_out[u, k, :, :width] = part[:, :width].astype(jnp.bfloat16)
                oo_out[u, k, :, width:] = rounded_symmetric(part[:, width:])
                oo_copy(d, i).start()

    def column(i):
        u = flip(v, i, var)
        for d in range(1, samp):
            cc_copy(d, i).wait_recv()
            oo_copy(d, i).wait_recv()
        cc, oc, oo = cc_own[u], oo_own[u, :, :width], oo_own[u, :, width:]
        for d in range(1, samp):
            p = flip(s, d, samp)
            cc = cc + cc_in[u, p].astype(jnp.float32)
            oc = oc + oo_in[u, p, :, :width].astype(jnp.float32)
            oo = oo + oo_in[u, p, :, width:].astype(jnp.float32)
        cc, oo = restored(cc), restored(oo)
        both = jnp.concatenate(
            [jnp.concatenate([cc, oc.T], axis=1), jnp.concatenate([oc, oo], axis=1)], axis=0)
        high = both.astype(jnp.bfloat16)
        low = (both - high.astype(jnp.float32)).astype(jnp.bfloat16)
        gram_parts = jnp.concatenate([high, low], axis=1)
        col = near_idx[u * samp + s]
        slot = own_slot[u * samp + s]
        wd = jnp.where(eye, 0.0, blk[col, slot])
        wo = blk[col, 1 - slot]
        dv = dia_ref[col]
        for step in range(STEPS):
            rounded = jnp.concatenate(
                [jnp.where(eye, dv, wd).astype(jnp.bfloat16), wo.astype(jnp.bfloat16)], axis=0)
            grad = jnp.dot(gram_parts, jnp.concatenate([rounded, rounded], axis=0),
                           preferred_element_type=jnp.float32)
            squares = jnp.sum(grad * rounded.astype(jnp.float32), axis=0, keepdims=True)
            terms = (squares / (2.0 * total_rows) - jnp.log(dv)
                     + penalty * jnp.sum(jnp.abs(wd) + jnp.abs(wo), axis=0, keepdims=True))
            acc[step:step + 1, :] += terms
            grad = grad / total_rows
            gd, go = grad[:width], grad[width:]
            wo = shrink(wo - step_length * go, step_length * penalty)
            wd = jnp.where(eye, 0.0, shrink(wd - step_length * gd, step_length * penalty))
            along = jnp.sum(jnp.where(eye, gd, 0.0), axis=0, keepdims=True)
            moved = dv - step_length * along
            dv = 0.5 * (moved + jnp.sqrt(moved * moved + 4.0 * step_length))
        fin_ref[s, u, 0] = wd.astype(jnp.bfloat16)
        fin_ref[s, u, 1] = wo.astype(jnp.bfloat16)
        tails_ref[s, pl.ds(u, 1), :] = dv

    def send_out(i, direct):
        for d in range(1, samp if direct else samp - 1):
            out_copy(d, i).start()

    def relay_copy(part, i):
        u = flip(v, i, var)
        near, to = flip(s, 1 + part, samp), flip(s, 2 - part, samp)
        return remote(fin_ref.at[near, u, part], fin_ref.at[near, u, part],
                      rel_s.at[part, i], rel_r.at[part, i], samp=to)

    def relay(i):
        for part in range(2):
            out_copy(1 + part, i).wait_recv()
            relay_copy(part, i).start()

    for i in range(1, var):
        ask_copy(i).start()
    acc[...] = jnp.zeros_like(acc)
    for x_load in x_loads:
        x_load.wait()
    start_cc(0)
    for i in range(1, var):
        ask_copy(i).wait_recv()
    ask[v] = want_ref[v]
    ask_load = pltpu.make_async_copy(ask, ask_s, ask_l)
    ask_load.start()
    ask_load.wait()

    def send_far(i, carry):
        u = flip(v, i, var)
        for k in range(samp):
            far[u, k] = panel(ask_s[u, 0, k])
        z_copy(i).start()
        return carry

    lax.fori_loop(1, var, send_far, 0)
    start_oo(0, lambda u, k: panel(wanted[u * samp + k]))
    lax.fori_loop(1, var, lambda i, c: (start_cc(i), c)[1], 0)
    blk_load.wait()

    def turn(i, carry):
        @pl.when(i < var)
        def _():
            z_copy(i).wait_recv()
            start_oo(i, lambda u, k: farz[u, k])

        column(i - 1)

        @pl.when(i < var - 1)
        def _():
            send_out(i - 1, False)

        @pl.when(i == var - 1)
        def _():
            send_out(i - 1, True)

        @pl.when(i > 2)
        def _():
            relay(i - 3)

        return carry

    lax.fori_loop(1, var + 1, turn, 0)

    tails_ref[s, var:, :] = acc[...]

    def tail_copy(d):
        return remote(tails_ref.at[s], tails_ref.at[s], tail_s.at[d], tail_r.at[d],
                      samp=flip(s, d, samp))

    def oz_copy(i):
        return remote(oz.at[v], oz.at[v], oz_s.at[i], oz_r.at[i], var=flip(v, i, var))

    for d in range(1, samp):
        tail_copy(d).start()
    send_out(var - 1, True)
    for d in range(1, samp):
        tail_copy(d).wait_recv()
    group = tails_ref[0, var:, :]
    for k in range(1, samp):
        group = group + tails_ref[k, var:, :]
    oz[v] = group
    for i in range(1, var):
        oz_copy(i).start()
    for i in range(1, var):
        oz_copy(i).wait_recv()
    whole = oz[0]
    for u in range(1, var):
        whole = whole + oz[u]
    obj_ref[...] = whole

    def finish(i, carry):
        for d in range(1, samp):
            cc_copy(d, i).wait_send()
            oo_copy(d, i).wait_send()
        for d in range(1, samp - 1):
            out_copy(d, i).wait_send()
        return carry

    def finish_relay(i, carry):
        for part in range(2):
            relay_copy(part, i).wait()
        return carry

    lax.fori_loop(0, var, finish, 0)
    lax.fori_loop(0, var - 2, finish_relay, 0)
    for i in range(var - 2, var):
        for d in range(1, samp - 1):
            out_copy(d, i).wait_recv()
        out_copy(samp - 1, i).wait()
    for d in range(1, samp):
        tail_copy(d).wait_send()
    for i in range(1, var):
        ask_copy(i).wait_send()
        z_copy(i).wait_send()
        oz_copy(i).wait_send()


def unpack_kernel(group, order, owner, rank, slot, fin_ref, tails_ref, whole_ref, out_ref, dia_ref, obj_ref):
    @pl.when(pl.program_id(0) == 0)
    def _():
        for step in range(STEPS):
            obj_ref[step] = jnp.sum(whole_ref[step:step + 1, :]) / order

    first = pl.program_id(0) * group
    for j in range(group):
        col = first + j
        k, u, at = rank[col], owner[col], slot[col]
        out_ref[j, 0] = fin_ref[k, u, at].astype(jnp.float32)
        out_ref[j, 1] = fin_ref[k, u, 1 - at].astype(jnp.float32)
        dia_ref[pl.ds(col, 1), :] = tails_ref[k, pl.ds(u, 1), :]


def column_body(observed, blocks, diagonal, pattern):
    cols, width = blocks.shape[0], blocks.shape[2]
    rows = observed.shape[0]
    var, samp = lax.axis_size("var"), lax.axis_size("samp")
    v = lax.axis_index("var")
    ids = jnp.arange(cols, dtype=jnp.int32)
    on_diag = pattern == (v * cols + ids)[:, None]
    off_row = jnp.sum(jnp.where(on_diag, 0, pattern), axis=1)
    diag_slot = jnp.where(on_diag[:, 1], 1, 0).astype(jnp.int32)
    owner = off_row // cols
    resident = off_row % cols
    earlier = (owner[None, :] == owner[:, None]) & (ids[None, :] < ids[:, None])
    rank = jnp.sum(earlier, axis=1).astype(jnp.int32)
    slot_index = owner * samp + rank
    match = slot_index[:, None] == ids[None, :]
    wanted = jnp.sum(jnp.where(match, resident[:, None], 0), axis=0)
    near_idx = jnp.sum(jnp.where(match, ids[:, None], 0), axis=0)
    own_slot = jnp.sum(jnp.where(match, diag_slot[:, None], 0), axis=0)
    want = jnp.pad(wanted.reshape(var, 1, samp), ((0, 0), (0, 0), (0, width - samp)))

    vmem = pl.BlockSpec(memory_space=pltpu.VMEM)
    smem = pl.BlockSpec(memory_space=pltpu.SMEM)
    hbm = pl.BlockSpec(memory_space=pl.ANY)
    dma = pltpu.SemaphoreType.DMA
    bf16, f32 = jnp.bfloat16, jnp.float32
    fin, tails, whole = pl.pallas_call(
        functools.partial(main_kernel, samp, var),
        out_shape=(
            jax.ShapeDtypeStruct((samp, var, 2, width, width), bf16),
            jax.ShapeDtypeStruct((samp, var + 8, width), f32),
            jax.ShapeDtypeStruct((8, width), f32),
        ),
        in_specs=[smem, smem, smem, vmem, hbm, hbm, vmem],
        out_specs=(vmem,) * 3,
        scratch_shapes=[
            pltpu.VMEM((cols, rows, width), observed.dtype),
            pltpu.VMEM(blocks.shape, f32),
            pltpu.VMEM((var, 1, width), jnp.int32),
            pltpu.SMEM((var, 1, width), jnp.int32),
            pltpu.VMEM((var, samp, rows, width), observed.dtype),
            pltpu.VMEM((var, samp, rows, width), observed.dtype),
            pltpu.VMEM((var, samp, width, width), bf16),
            pltpu.VMEM((var, samp, width, width), bf16),
            pltpu.VMEM((var, width, width), f32),
            pltpu.VMEM((var, samp, width, 2 * width), bf16),
            pltpu.VMEM((var, samp, width, 2 * width), bf16),
            pltpu.VMEM((var, width, 2 * width), f32),
            pltpu.VMEM((var, 8, width), f32),
            pltpu.VMEM((8, width), f32),
            dma((cols + 1,)), dma((var,)), dma((var,)), dma,
            dma((samp, var)), dma((samp, var)), dma((var,)), dma((var,)),
            dma((samp, var)), dma((samp, var)), dma((samp, var)), dma((samp, var)),
            dma((2, var)), dma((2, var)), dma((samp,)), dma((samp,)), dma((var,)), dma((var,)),
        ],
        compiler_params=pltpu.CompilerParams(collective_id=0, has_side_effects=True),
        name="columns",
    )(near_idx, wanted, own_slot, want, observed, blocks, diagonal.reshape(cols, 1, width))

    group = 4
    new_blocks, new_diagonal, objective = pl.pallas_call(
        functools.partial(unpack_kernel, group, float(cols * width * var)),
        out_shape=(
            jax.ShapeDtypeStruct(blocks.shape, jnp.float32),
            jax.ShapeDtypeStruct((cols, width), jnp.float32),
            jax.ShapeDtypeStruct((STEPS,), jnp.float32),
        ),
        grid=(cols // group,),
        in_specs=[smem, smem, smem, vmem, vmem, vmem],
        out_specs=(
            pl.BlockSpec((group, 2, width, width), lambda g: (g, 0, 0, 0)),
            pl.BlockSpec((cols, width), lambda g: (0, 0)),
            smem,
        ),
        name="unpack",
    )(owner, rank, diag_slot, fin, tails, whole)
    return new_blocks, new_diagonal.reshape(-1), objective


def advance(diag_block, off_block, diag_values, grad_diag, grad_off, diag_mask, total_rows):
    grad_diag = grad_diag / total_rows
    grad_off = grad_off / total_rows
    new_off = shrink(off_block - step_length * grad_off, step_length * penalty)
    new_diag_block = jnp.where(
        diag_mask, 0.0, shrink(diag_block - step_length * grad_diag, step_length * penalty)
    )
    along = jnp.sum(jnp.where(diag_mask, grad_diag, 0.0), axis=1)
    moved = diag_values - step_length * along
    new_values = 0.5 * (moved + jnp.sqrt(moved * moved + 4.0 * step_length))
    return (new_diag_block, new_off, new_values)


def body(observed, blocks, diagonal, pattern):
    col_count = blocks.shape[0]
    block_width = blocks.shape[2]
    sample_rows = observed.shape[0]
    var_count = lax.axis_size("var")
    samp_count = lax.axis_size("samp")
    capacity = max(2, -(-col_count // var_count))
    total_rows = sample_rows * samp_count
    matrix_order = col_count * block_width * var_count
    var_index = lax.axis_index("var")
    column_ids = jnp.arange(col_count, dtype=jnp.int32)
    columns = var_index * col_count + column_ids
    on_diag = pattern == columns[:, None]
    off_row = jnp.sum(jnp.where(on_diag, 0, pattern), axis=1)
    owner_index = off_row // col_count
    resident_block = off_row % col_count
    earlier = (owner_index[None, :] == owner_index[:, None]) & (
        column_ids[None, :] < column_ids[:, None]
    )
    position_rank = jnp.sum(earlier, axis=1)
    slot_index = owner_index * capacity + position_rank
    all_slots = jnp.arange(var_count * capacity, dtype=jnp.int32)
    slot_match = slot_index[:, None] == all_slots[None, :]
    wanted = jnp.sum(jnp.where(slot_match, resident_block[:, None], 0), axis=0)
    asked_blocks = lax.all_to_all(wanted, "var", split_axis=0, concat_axis=0, tiled=True)
    nearby_panels = observed.reshape(sample_rows, col_count, block_width)
    outgoing = jnp.take(nearby_panels, asked_blocks, axis=1)
    arrived = lax.all_to_all(outgoing, "var", split_axis=1, concat_axis=1, tiled=True)
    distant_panels = jnp.take(arrived, slot_index, axis=1)
    diag_mask = jnp.eye(block_width, dtype=bool)
    flags = on_diag[:, :, None, None]
    diag_block = jnp.sum(jnp.where(flags, blocks, 0.0), axis=1)
    diag_block = jnp.where(diag_mask, 0.0, diag_block)
    off_block = jnp.sum(jnp.where(flags, 0.0, blocks), axis=1)
    diag_values = diagonal.reshape(col_count, block_width)
    samp_first = (lax.axis_index("samp") == 0).astype(jnp.float32)
    objective_parts = []
    for iteration in range(STEPS):
        full_diag = jnp.where(diag_mask, diag_values[:, None, :], diag_block)
        product = jnp.einsum(
            "qlh,lhy->qly",
            nearby_panels,
            full_diag.astype(jnp.bfloat16),
            preferred_element_type=jnp.float32,
        )
        product = product + jnp.einsum(
            "qlh,lhy->qly",
            distant_panels,
            off_block.astype(jnp.bfloat16),
            preferred_element_type=jnp.float32,
        )
        squares = jnp.sum(product * product)
        local_terms = -jnp.sum(jnp.log(diag_values)) + penalty * (
            jnp.sum(jnp.abs(diag_block)) + jnp.sum(jnp.abs(off_block))
        )
        part_value = (squares / (2.0 * total_rows) + samp_first * local_terms) / matrix_order
        objective_parts.append(part_value)
        lower_precision_product = product.astype(jnp.bfloat16)
        grad_diag = jnp.einsum(
            "rei,reo->eio",
            nearby_panels,
            lower_precision_product,
            preferred_element_type=jnp.float32,
        )
        grad_off = jnp.einsum(
            "rei,reo->eio",
            distant_panels,
            lower_precision_product,
            preferred_element_type=jnp.float32,
        )
        grad_diag, grad_off = lax.psum((grad_diag, grad_off), "samp")
        diag_block, off_block, diag_values = advance(
            diag_block, off_block, diag_values, grad_diag, grad_off, diag_mask, total_rows
        )
    objective = lax.psum(jnp.stack(objective_parts), ("samp", "var"))
    new_blocks = jnp.where(flags, diag_block[:, None], off_block[:, None])
    return (new_blocks, diag_values.reshape(-1), objective)


def power_of_two(count):
    return count & (count - 1) == 0


def whole_body(observed, blocks, diagonal, pattern):
    cols = blocks.shape[0]
    var, samp = lax.axis_size("var"), lax.axis_size("samp")
    exact = samp == 4 and samp * var == cols and cols % 4 == 0 and var % 8 == 0 and blocks.shape[2] == 128
    if exact and power_of_two(samp) and power_of_two(var):
        return column_body(observed, blocks, diagonal, pattern)
    return body(observed, blocks, diagonal, pattern)


def solution(mesh):
    placed = (P("samp", "var"), P("var", None, None, None), P("var"), P("var", None))
    return jax.shard_map(
        whole_body,
        mesh=mesh,
        in_specs=placed,
        out_specs=(P("var", None, None, None), P("var"), P()),
        check_vma=False,
    )
```

profile of v0, /device:TPU:0, one launch (start us, length us, event | category | flops | bytes accessed | tf_op | source)
XLA Modules:
  0.0 84.1 jit_solution(6754643952061920409)
XLA Ops:
  0.6 0.7 select_reduce_fusion.3
  1.3 0.7 broadcast_compare_fusion
  2.0 0.0 copy-start.1
  2.1 0.0 copy-start.2
  2.1 0.2 convert_reduce_fusion.rank
  2.3 0.0 copy-start.3
  2.3 0.6 select_reduce_fusion
  2.9 0.0 copy-start
  2.9 0.1 reshape.75
  3.0 0.6 pad.4.want_ref
  3.6 0.0 copy-done
  3.6 75.2 %columns.1 = (bf16[4,8,2,128,128]{4,3,2,1,0:T(8,128)(2,1)}, f32[4,16,128]{2,1,0:T(8,128)}, f32[8,128]{1,0:T(8,128)}) custom-call(s32[32]{0:T(128)} %get-tuple-element.17.near_idx, s32[32]{0:T(128)} %copy-done, s32[32]{0:T(128)} %get-tuple-element.15.own_slot, s32[8,1,128]{2,1,0:T(1,128)} %pad.4.want_ref, bf16[256,4096]{1,0:T(8,128)(2,1)} %x_hbm.1, ...), custom_call_target="tpu_custom_call" | custom-call | tf_op jit(solution)/shard_map/columns/pallas_call | solution.py:342
  78.7 0.0 copy-done.1
  78.8 0.0 copy-done.2
  78.8 0.0 copy-done.3
  78.8 5.3 %unpack.1 = (f32[32,2,128,128]{3,2,1,0:T(8,128)}, f32[32,128]{1,0:T(8,128)}, f32[2]{0:T(128)}) custom-call(s32[32]{0:T(128)} %copy-done.2, s32[32]{0:T(128)} %copy-done.3, s32[32]{0:T(128)} %copy-done.1, bf16[4,8,2,128,128]{4,3,2,1,0:T(8,128)(2,1)} %get-tuple-element.9.fin_ref, f32[4,16,128]{2,1,0:T(8,128)} %get-tuple-element.10.tails_ref, ...), custom_call_target="tpu_custom_call" | custom-call | tf_op jit(solution)/shard_map/unpack/pallas_call | solution.py:376
  (4 shorter events, 0.0 us)
Async XLA Ops:
  2.0 76.7 %copy-start.1 = (s32[32]{0:T(128)}, s32[32]{0:T(128)S(1)}, u32[]{:S(2)}) copy-start(s32[32]{0:T(128)S(1)} %fusion.1.slot) | copy-start | bytes 388
  2.1 76.7 %copy-start.2 = (s32[32]{0:T(128)}, s32[32]{0:T(128)S(1)}, u32[]{:S(2)}) copy-start(s32[32]{0:T(128)S(1)} %get-tuple-element.19.owner) | copy-start | bytes 388
  2.3 76.5 %copy-start.3 = (s32[32]{0:T(128)}, s32[32]{0:T(128)S(1)}, u32[]{:S(2)}) copy-start(s32[32]{0:T(128)S(1)} %convert_reduce_fusion.rank) | copy-start | bytes 388
  2.9 0.7 copy-start
where the time goes:
time: 84.4 us; the launch traced here: 84.1 us
  Pallas kernels  80.5 us (95%)
  other arithmetic  2.2 us (3%)
    pallas_call x1, Pallas kernels, column_body(): pl.pallas_call(functools.partial(main_kernel, samp, var), out_shape=(jax....  75.2 us
    pallas_call x1, Pallas kernels, column_body(): pl.pallas_call(functools.partial(unpack_kernel, group, float(cols * width...  5.35 us

commit v1 on v0

v1 whole, which is shorter than its diff:
```python
import functools

import jax
import jax.numpy as jnp
from jax import lax
from jax.experimental import pallas as pl
from jax.experimental.pallas import tpu as pltpu
from jax.sharding import PartitionSpec as P

STEPS = 2


step_length = 0.5
penalty = 0.5
MESH = pl.DeviceIdType.MESH


def shrink(moved, level):
    return moved - jnp.clip(moved, -level, level)


def flip(index, offset, count):
    out, bit = 0, 1
    while bit < count:
        out = out + ((index // bit + offset // bit) % 2) * bit
        bit *= 2
    return out


def inner_chip(v):
    return ((v // 2 + 1) // 2) % 2


def partner(v, b, k, var):
    half = var // 2
    close = half + 2 * inner_chip(v)
    distant = 2 * half + 2 - close
    high, low = k // 2, k % 2
    return (0, 1, 2 + high, close + low, 3 - high, distant + low, distant + 1 - low, close + 1 - low)[b]


def send_rank(i, n, samp, half):
    if isinstance(i, int) and i < half:
        return (n + (i - 2) * (samp // 2)) % samp
    return 2 * n + i % 2 if n < 2 else 2 * (n - 2) + 1 - i % 2


def main_kernel(samp, var, pat_hbm, x_hbm, blk_hbm, dia_hbm,
                fin_ref, tails_ref, obj_ref, tab_ref,
                pat_ref, x, blk, dia_ref, tab, ask, ask_s, far, farz, cc_out, cc_in, cc_own, cc_diag,
                oo_out, oo_in, oc_own, oo_own, oo_diag, oz, acc,
                load, tab_l, ask_ss, ask_rs, ask_l, cc_s, cc_r, z_s, z_r, oo_s, oo_r, out_s, out_r,
                rel_s, rel_r, tail_s, tail_r, oz_s, oz_r):
    s = lax.axis_index("samp")
    v = lax.axis_index("var")
    inner = inner_chip(v)
    rows, width = x.shape[1], x.shape[2]
    half = var // 2
    fold_rows = width // 2
    total_rows = rows * samp
    over_first = (((0,), (0,)), ((), ()))

    cols = x.shape[0]
    bits = cols.bit_length() - 1
    barrier = pltpu.get_barrier_semaphore()
    for i in range(1, var):
        pl.semaphore_signal(barrier, inc=1, device_id={"var": flip(v, i, var)}, device_id_type=MESH)
    for d in range(1, samp):
        pl.semaphore_signal(barrier, inc=1, device_id={"samp": flip(s, d, samp)}, device_id_type=MESH)

    pat_load = pltpu.make_async_copy(pat_hbm, pat_ref, load.at[cols + 1])
    pat_load.start()
    x_loads = [
        pltpu.make_async_copy(x_hbm.at[:, l * width:(l + 1) * width], x.at[l], load.at[l])
        for l in range(cols)
    ]
    for x_load in x_loads:
        x_load.start()
    blk_load = pltpu.make_async_copy(blk_hbm, blk, load.at[cols])
    dia_load = pltpu.make_async_copy(dia_hbm, dia_ref, load.at[cols + 2])

    pat_load.wait()
    first, second = pat_ref[0:1, :], pat_ref[1:2, :]
    ids = lax.broadcasted_iota(jnp.int32, (1, cols), 1)
    lead = first == v * cols + ids
    off_row = jnp.where(lead, second, first)
    owner = lax.shift_right_logical(off_row, bits)
    entry = (off_row & (cols - 1)) + ids * cols + jnp.where(lead, 0, cols * cols)
    below = lax.broadcasted_iota(jnp.int32, (cols, cols), 0)
    across = lax.broadcasted_iota(jnp.int32, (cols, cols), 1)
    wide = jnp.broadcast_to(owner, (cols, cols))
    down = jnp.sum(jnp.where(below == across, wide, 0), axis=1, keepdims=True)
    rank = jnp.sum(jnp.where((down == wide) & (below < across), 1, 0), axis=0, keepdims=True)
    mine = lax.broadcasted_iota(jnp.int32, (var, cols), 0) == owner
    lanes = lax.broadcasted_iota(jnp.int32, (var, width), 1)
    table = jnp.zeros((var, width), jnp.int32)
    for k in range(samp):
        picked = jnp.sum(jnp.where(mine & (rank == k), entry, 0), axis=1, keepdims=True)
        table = jnp.where(lanes == k, picked, table)
    for u in range(var):
        tab_ref[u] = table[u:u + 1, :]
    tab_load = pltpu.make_async_copy(tab_ref, tab, tab_l)
    tab_load.start()

    pl.semaphore_wait(barrier, samp + var - 2)

    def remote(src, dst, send, recv, **where):
        return pltpu.make_async_remote_copy(
            src_ref=src, dst_ref=dst, send_sem=send, recv_sem=recv,
            device_id=where, device_id_type=MESH)

    def ask_copy(i):
        u = flip(v, i, var)
        return remote(tab_ref.at[u], ask.at[v], ask_ss.at[i], ask_rs.at[i], var=u)

    def ask_load(i):
        u = flip(v, i, var)
        return pltpu.make_async_copy(ask.at[u], ask_s.at[u], ask_l.at[i])

    def z_copy(i, k):
        u = flip(v, i, var)
        return remote(far.at[u, k], farz.at[v, k], z_s.at[i, k], z_r.at[i, k], var=u)

    def cc_copy(b, k):
        return remote(cc_out.at[b, k], cc_in.at[b, s], cc_s.at[b, k], cc_r.at[b, s], samp=k)

    def oo_copy(b, k):
        return remote(oo_out.at[b, k], oo_in.at[b, s], oo_s.at[b, k], oo_r.at[b, s], samp=k)

    def cc_arrival(b, k):
        return remote(cc_out.at[b, k], cc_in.at[b, k], cc_s.at[b, k], cc_r.at[b, k], samp=k)

    def oo_arrival(b, k):
        return remote(oo_out.at[b, k], oo_in.at[b, k], oo_s.at[b, k], oo_r.at[b, k], samp=k)

    def out_copy(d, b):
        return remote(fin_ref.at[s, b], fin_ref.at[s, b], out_s.at[d, b], out_r.at[d, b],
                      samp=flip(s, d, samp))

    def near_panel(u, k):
        return x[lax.shift_right_logical(tab[u, 0, k], bits) & (cols - 1)]

    def gram(left, right):
        return lax.dot_general(left, right, over_first, preferred_element_type=jnp.float32)

    row_at = lax.broadcasted_iota(jnp.int32, (width, width), 0)
    col_at = lax.broadcasted_iota(jnp.int32, (width, width), 1)
    eye = row_at == col_at
    fold_row = lax.broadcasted_iota(jnp.int32, (fold_rows, width), 0)
    fold_col = lax.broadcasted_iota(jnp.int32, (fold_rows, width), 1)
    from_top = fold_col >= fold_row + fold_rows
    own_top = (fold_col < fold_rows) & (fold_col >= fold_row)
    note_row = lax.broadcasted_iota(jnp.int32, (16, width), 0)

    def folded(part):
        return jnp.where(from_top, pltpu.roll(part[:fold_rows], fold_rows, 1), part[fold_rows:])

    def unfolded(half_block, diag):
        turned = pltpu.roll(half_block, fold_rows, 1)
        mirror = jnp.concatenate([half_block, turned], axis=0).T
        top = jnp.where(own_top, turned, mirror[fold_rows:])
        bottom = jnp.where(from_top, mirror[:fold_rows], half_block)
        return jnp.where(eye, diag, jnp.concatenate([top, bottom], axis=0))

    def diagonal_of(part):
        return jnp.sum(jnp.where(eye, part, 0.0), axis=0, keepdims=True)

    def note_of(diag):
        high = diag.astype(jnp.bfloat16).astype(jnp.float32)
        return jnp.where(note_row == 0, high, jnp.where(note_row == 1, diag - high, 0.0))

    def start_cc(b):
        for k in range(samp):
            u = flip(v, partner(v, b, k, var), var)
            c = near_panel(u, k)
            part = gram(c, c)
            short, diag = folded(part), diagonal_of(part)
            cc_out[b, k, :fold_rows] = short.astype(jnp.bfloat16)
            cc_out[b, k, fold_rows:] = note_of(diag).astype(jnp.bfloat16)

            @pl.when(s == k)
            def _():
                cc_own[b] = short
                cc_diag[b] = diag

            @pl.when(s != k)
            def _():
                cc_copy(b, k).start()

    def start_oo(b, ranks, far_panel):
        for k in ranks:
            u = flip(v, partner(v, b, k, var), var)
            o = far_panel(u, k)
            part = gram(o, jnp.concatenate([near_panel(u, k), o], axis=1))
            cross, own = part[:, :width], part[:, width:]
            short, diag = folded(own), diagonal_of(own)
            oo_out[b, k, :width] = cross.astype(jnp.bfloat16)
            oo_out[b, k, width:width + fold_rows] = short.astype(jnp.bfloat16)
            oo_out[b, k, width + fold_rows:] = note_of(diag).astype(jnp.bfloat16)

            @pl.when(s == k)
            def _():
                oc_own[b] = cross
                oo_own[b] = short
                oo_diag[b] = diag

            @pl.when(s != k)
            def _():
                oo_copy(b, k).start()

    def arrived(b, ranks):
        for k in ranks:
            z_copy(partner(v, b, k, var), k).wait_recv()

    def note_sum(note):
        note = note.astype(jnp.float32)
        return note[0:1] + note[1:2]

    def column(b):
        for d in range(1, samp):
            cc_arrival(b, flip(s, d, samp)).wait_recv()
            oo_arrival(b, flip(s, d, samp)).wait_recv()
        cc, oc, oo = cc_own[b], oc_own[b], oo_own[b]
        cc_d, oo_d = cc_diag[b], oo_diag[b]
        for d in range(1, samp):
            p = flip(s, d, samp)
            cc = cc + cc_in[b, p, :fold_rows].astype(jnp.float32)
            cc_d = cc_d + note_sum(cc_in[b, p, fold_rows:])
            oc = oc + oo_in[b, p, :width].astype(jnp.float32)
            oo = oo + oo_in[b, p, width:width + fold_rows].astype(jnp.float32)
            oo_d = oo_d + note_sum(oo_in[b, p, width + fold_rows:])
        cc, oo = unfolded(cc, cc_d), unfolded(oo, oo_d)
        both = jnp.concatenate(
            [jnp.concatenate([cc, oc.T], axis=1), jnp.concatenate([oc, oo], axis=1)], axis=0)
        high = both.astype(jnp.bfloat16)
        low = (both - high.astype(jnp.float32)).astype(jnp.bfloat16)
        gram_parts = jnp.concatenate([high, low], axis=1)
        u = flip(v, partner(v, b, s, var), var)
        value = tab[u, 0, s]
        col = lax.shift_right_logical(value, bits) & (cols - 1)
        slot = lax.shift_right_logical(value, 2 * bits) & 1
        wd = jnp.where(eye, 0.0, blk[col, slot])
        wo = blk[col, 1 - slot]
        dv = dia_ref[col]
        for step in range(STEPS):
            rounded = jnp.concatenate(
                [jnp.where(eye, dv, wd).astype(jnp.bfloat16), wo.astype(jnp.bfloat16)], axis=0)
            grad = jnp.dot(gram_parts, jnp.concatenate([rounded, rounded], axis=0),
                           preferred_element_type=jnp.float32)
            squares = jnp.sum(grad * rounded.astype(jnp.float32), axis=0, keepdims=True)
            terms = (squares / (2.0 * total_rows) - jnp.log(dv)
                     + penalty * jnp.sum(jnp.abs(wd) + jnp.abs(wo), axis=0, keepdims=True))
            acc[step:step + 1, :] += terms
            grad = grad / total_rows
            gd, go = grad[:width], grad[width:]
            wo = shrink(wo - step_length * go, step_length * penalty)
            wd = jnp.where(eye, 0.0, shrink(wd - step_length * gd, step_length * penalty))
            along = jnp.sum(jnp.where(eye, gd, 0.0), axis=0, keepdims=True)
            moved = dv - step_length * along
            dv = 0.5 * (moved + jnp.sqrt(moved * moved + 4.0 * step_length))
        fin_ref[s, b, 0] = wd.astype(jnp.bfloat16)
        fin_ref[s, b, 1] = wo.astype(jnp.bfloat16)
        tails_ref[s, pl.ds(b, 1), :] = dv

    def send_out(b, direct):
        for d in range(1, samp if direct else samp - 1):
            out_copy(d, b).start()

    def relay_copy(part, b):
        near, to = flip(s, 1 + part, samp), flip(s, 2 - part, samp)
        return remote(fin_ref.at[near, b, part], fin_ref.at[near, b, part],
                      rel_s.at[part, b], rel_r.at[part, b], samp=to)

    def relay(b):
        for part in range(2):
            out_copy(1 + part, b).wait_recv()
            relay_copy(part, b).start()

    close = half + 2 * inner
    distant = 2 * half + 2 - close
    asks = [2, 3, close, close + 1, 1, distant, distant + 1]
    for i in asks:
        ask_copy(i).start()
    acc[...] = jnp.zeros_like(acc)
    for x_load in x_loads:
        x_load.wait()
    blk_load.start()
    dia_load.start()
    tab_load.wait()
    start_cc(0)

    def learn(offsets):
        for i in offsets:
            ask_copy(i).wait_recv()
            ask_load(i).start()
        for i in offsets:
            ask_load(i).wait()

    def send_panel(i, k):
        u = flip(v, i, var)
        far[u, k] = x[ask_s[u, 0, k] & (cols - 1)]
        z_copy(i, k).start()

    def send_across():
        for n in range(samp):
            for i in (close, distant, close + 1, distant + 1):
                send_panel(i, send_rank(i, n, samp, half))

    learn([2, 3, close, close + 1])

    @pl.when(inner == 1)
    def _():
        for i in (close, close + 1):
            send_panel(i, send_rank(i, 0, samp, half))

    for n in range(samp):
        for i in (2, 3):
            send_panel(i, send_rank(i, n, samp, half))
    learn([1, distant, distant + 1])

    @pl.when(inner == 1)
    def _():
        for i in (distant, distant + 1):
            send_panel(i, send_rank(i, 0, samp, half))
        for n in range(1, samp):
            for i in (close, distant, close + 1, distant + 1):
                send_panel(i, send_rank(i, n, samp, half))

    for k in range(samp):
        send_panel(1, k)

    every = range(samp)
    start_oo(0, every, lambda u, k: x[tab[u, 0, k] & (cols - 1)])
    start_cc(1)

    def from_var(u, k):
        return farz[u, k]

    def take(b, ranks=every):
        arrived(b, ranks)
        start_oo(b, ranks, from_var)

    def settle(b, direct=False):
        column(b)
        send_out(b, direct)

    last = var - 1
    take(1)
    for b in range(2, var):
        start_cc(b)
    blk_load.wait()
    dia_load.wait()
    settle(0)
    take(2)
    settle(1)
    arrived(3, every)

    @pl.when(inner == 0)
    def _():
        send_across()

    start_oo(3, every, from_var)
    settle(2)
    relay(0)
    relay(1)
    take(4)
    settle(3)
    relay(2)
    take(5)
    settle(4)
    relay(3)
    settle(5)
    relay(4)
    take(6)
    relay(5)
    settle(6, True)
    take(last, range(samp // 2))
    take(last, range(samp // 2, samp))
    column(last)

    tails_ref[s, var:, :] = acc[...]

    def tail_copy(d):
        return remote(tails_ref.at[s], tails_ref.at[s], tail_s.at[d], tail_r.at[d],
                      samp=flip(s, d, samp))

    def oz_copy(i):
        return remote(oz.at[v], oz.at[v], oz_s.at[i], oz_r.at[i], var=flip(v, i, var))

    for d in range(1, samp):
        tail_copy(d).start()
    send_out(last, True)
    for d in range(1, samp):
        tail_copy(d).wait_recv()
    group = tails_ref[0, var:, :]
    for k in range(1, samp):
        group = group + tails_ref[k, var:, :]
    oz[v] = group
    for i in range(1, var):
        oz_copy(i).start()

    def finish(b, carry):
        for d in range(1, samp - 1):
            out_copy(d, b).wait_send()
        return carry

    def finish_relay(b, carry):
        for part in range(2):
            relay_copy(part, b).wait()
        return carry

    lax.fori_loop(0, var, finish, 0)
    for k in range(samp):
        @pl.when(s != k)
        def _():
            def sent(b, carry):
                cc_copy(b, k).wait_send()
                oo_copy(b, k).wait_send()
                return carry

            lax.fori_loop(0, var, sent, 0)
    lax.fori_loop(0, var - 2, finish_relay, 0)
    for b in range(var - 2, var):
        for d in range(1, samp - 1):
            out_copy(d, b).wait_recv()
        out_copy(samp - 1, b).wait()
    for d in range(1, samp):
        tail_copy(d).wait_send()
    for i in range(1, var):
        ask_copy(i).wait_send()
        for k in range(samp):
            z_copy(i, k).wait_send()
    for i in range(1, var):
        oz_copy(i).wait()
    whole = oz[0]
    for u in range(1, var):
        whole = whole + oz[u]
    obj_ref[...] = whole


def unpack_kernel(samp, var, order, bits, table, fin_ref, tails_ref, whole_ref,
                  out_hbm, dia_ref, obj_ref, stage, sem):
    v = lax.axis_index("var")
    last = (1 << bits) - 1
    copies = []
    for b in range(var):
        for k in range(samp):
            value = table[flip(v, partner(v, b, k, var), var), 0, k]
            col = lax.shift_right_logical(value, bits) & last
            slot = lax.shift_right_logical(value, 2 * bits) & 1
            stage[b, k, slot] = fin_ref[k, b, 0].astype(jnp.float32)
            stage[b, k, 1 - slot] = fin_ref[k, b, 1].astype(jnp.float32)
            copy = pltpu.make_async_copy(stage.at[b, k], out_hbm.at[col], sem.at[b, k])
            copy.start()
            copies.append(copy)
            dia_ref[pl.ds(col, 1), :] = tails_ref[k, b:b + 1, :]
    for step in range(STEPS):
        obj_ref[step] = jnp.sum(whole_ref[step:step + 1, :]) / order
    for copy in copies:
        copy.wait()


def column_body(observed, blocks, diagonal, pattern):
    cols, width = blocks.shape[0], blocks.shape[2]
    rows = observed.shape[0]
    var, samp = lax.axis_size("var"), lax.axis_size("samp")
    bits = cols.bit_length() - 1

    vmem = pl.BlockSpec(memory_space=pltpu.VMEM)
    smem = pl.BlockSpec(memory_space=pltpu.SMEM)
    hbm = pl.BlockSpec(memory_space=pltpu.HBM)
    dma = pltpu.SemaphoreType.DMA
    bf16, f32 = jnp.bfloat16, jnp.float32
    fold, late_rows = width // 2 + 16, width + width // 2 + 16
    fin, tails, whole, table = pl.pallas_call(
        functools.partial(main_kernel, samp, var),
        out_shape=(
            jax.ShapeDtypeStruct((samp, var, 2, width, width), bf16),
            jax.ShapeDtypeStruct((samp, var + 8, width), f32),
            jax.ShapeDtypeStruct((8, width), f32),
            jax.ShapeDtypeStruct((var, 1, width), jnp.int32),
        ),
        in_specs=[hbm] * 4,
        out_specs=(vmem,) * 4,
        scratch_shapes=[
            pltpu.VMEM((2, cols), jnp.int32),
            pltpu.VMEM((cols, rows, width), observed.dtype),
            pltpu.VMEM(blocks.shape, f32),
            pltpu.VMEM((cols, 1, width), f32),
            pltpu.SMEM((var, 1, width), jnp.int32),
            pltpu.VMEM((var, 1, width), jnp.int32),
            pltpu.SMEM((var, 1, width), jnp.int32),
            pltpu.VMEM((var, samp, rows, width), observed.dtype),
            pltpu.VMEM((var, samp, rows, width), observed.dtype),
            pltpu.VMEM((var, samp, fold, width), bf16),
            pltpu.VMEM((var, samp, fold, width), bf16),
            pltpu.VMEM((var, width // 2, width), f32),
            pltpu.VMEM((var, 1, width), f32),
            pltpu.VMEM((var, samp, late_rows, width), bf16),
            pltpu.VMEM((var, samp, late_rows, width), bf16),
            pltpu.VMEM((var, width, width), f32),
            pltpu.VMEM((var, width // 2, width), f32),
            pltpu.VMEM((var, 1, width), f32),
            pltpu.VMEM((var, 8, width), f32),
            pltpu.VMEM((8, width), f32),
            dma((cols + 3,)), dma, dma((var,)), dma((var,)), dma((var,)),
            dma((var, samp)), dma((var, samp)), dma((var, samp)), dma((var, samp)),
            dma((var, samp)), dma((var, samp)), dma((samp, var)), dma((samp, var)),
            dma((2, var)), dma((2, var)), dma((samp,)), dma((samp,)), dma((var,)), dma((var,)),
        ],
        compiler_params=pltpu.CompilerParams(
            collective_id=0, has_side_effects=True, vmem_limit_bytes=40 * 2 ** 20),
        name="columns",
    )(*(pltpu.with_memory_space_constraint(array, pltpu.HBM)
        for array in (pattern.T, observed, blocks, diagonal.reshape(cols, 1, width))))

    new_blocks, new_diagonal, objective = pl.pallas_call(
        functools.partial(unpack_kernel, samp, var, float(cols * width * var), bits),
        out_shape=(
            jax.ShapeDtypeStruct(blocks.shape, f32),
            jax.ShapeDtypeStruct((cols, width), f32),
            jax.ShapeDtypeStruct((STEPS,), f32),
        ),
        in_specs=[smem, vmem, vmem, vmem],
        out_specs=(hbm, vmem, smem),
        scratch_shapes=[
            pltpu.VMEM((var, samp, 2, width, width), f32),
            dma((var, samp)),
        ],
        compiler_params=pltpu.CompilerParams(vmem_limit_bytes=16 * 2 ** 20),
        name="unpack",
    )(table, fin, tails, whole)
    return new_blocks, new_diagonal.reshape(-1), objective


def advance(diag_block, off_block, diag_values, grad_diag, grad_off, diag_mask, total_rows):
    grad_diag = grad_diag / total_rows
    grad_off = grad_off / total_rows
    new_off = shrink(off_block - step_length * grad_off, step_length * penalty)
    new_diag_block = jnp.where(
        diag_mask, 0.0, shrink(diag_block - step_length * grad_diag, step_length * penalty)
    )
    along = jnp.sum(jnp.where(diag_mask, grad_diag, 0.0), axis=1)
    moved = diag_values - step_length * along
    new_values = 0.5 * (moved + jnp.sqrt(moved * moved + 4.0 * step_length))
    return (new_diag_block, new_off, new_values)


def body(observed, blocks, diagonal, pattern):
    col_count = blocks.shape[0]
    block_width = blocks.shape[2]
    sample_rows = observed.shape[0]
    var_count = lax.axis_size("var")
    samp_count = lax.axis_size("samp")
    capacity = max(2, -(-col_count // var_count))
    total_rows = sample_rows * samp_count
    matrix_order = col_count * block_width * var_count
    var_index = lax.axis_index("var")
    column_ids = jnp.arange(col_count, dtype=jnp.int32)
    columns = var_index * col_count + column_ids
    on_diag = pattern == columns[:, None]
    off_row = jnp.sum(jnp.where(on_diag, 0, pattern), axis=1)
    owner_index = off_row // col_count
    resident_block = off_row % col_count
    earlier = (owner_index[None, :] == owner_index[:, None]) & (
        column_ids[None, :] < column_ids[:, None]
    )
    position_rank = jnp.sum(earlier, axis=1)
    slot_index = owner_index * capacity + position_rank
    all_slots = jnp.arange(var_count * capacity, dtype=jnp.int32)
    slot_match = slot_index[:, None] == all_slots[None, :]
    wanted = jnp.sum(jnp.where(slot_match, resident_block[:, None], 0), axis=0)
    asked_blocks = lax.all_to_all(wanted, "var", split_axis=0, concat_axis=0, tiled=True)
    nearby_panels = observed.reshape(sample_rows, col_count, block_width)
    outgoing = jnp.take(nearby_panels, asked_blocks, axis=1)
    arrived = lax.all_to_all(outgoing, "var", split_axis=1, concat_axis=1, tiled=True)
    distant_panels = jnp.take(arrived, slot_index, axis=1)
    diag_mask = jnp.eye(block_width, dtype=bool)
    flags = on_diag[:, :, None, None]
    diag_block = jnp.sum(jnp.where(flags, blocks, 0.0), axis=1)
    diag_block = jnp.where(diag_mask, 0.0, diag_block)
    off_block = jnp.sum(jnp.where(flags, 0.0, blocks), axis=1)
    diag_values = diagonal.reshape(col_count, block_width)
    samp_first = (lax.axis_index("samp") == 0).astype(jnp.float32)
    objective_parts = []
    for iteration in range(STEPS):
        full_diag = jnp.where(diag_mask, diag_values[:, None, :], diag_block)
        product = jnp.einsum(
            "qlh,lhy->qly",
            nearby_panels,
            full_diag.astype(jnp.bfloat16),
            preferred_element_type=jnp.float32,
        )
        product = product + jnp.einsum(
            "qlh,lhy->qly",
            distant_panels,
            off_block.astype(jnp.bfloat16),
            preferred_element_type=jnp.float32,
        )
        squares = jnp.sum(product * product)
        local_terms = -jnp.sum(jnp.log(diag_values)) + penalty * (
            jnp.sum(jnp.abs(diag_block)) + jnp.sum(jnp.abs(off_block))
        )
        part_value = (squares / (2.0 * total_rows) + samp_first * local_terms) / matrix_order
        objective_parts.append(part_value)
        lower_precision_product = product.astype(jnp.bfloat16)
        grad_diag = jnp.einsum(
            "rei,reo->eio",
            nearby_panels,
            lower_precision_product,
            preferred_element_type=jnp.float32,
        )
        grad_off = jnp.einsum(
            "rei,reo->eio",
            distant_panels,
            lower_precision_product,
            preferred_element_type=jnp.float32,
        )
        grad_diag, grad_off = lax.psum((grad_diag, grad_off), "samp")
        diag_block, off_block, diag_values = advance(
            diag_block, off_block, diag_values, grad_diag, grad_off, diag_mask, total_rows
        )
    objective = lax.psum(jnp.stack(objective_parts), ("samp", "var"))
    new_blocks = jnp.where(flags, diag_block[:, None], off_block[:, None])
    return (new_blocks, diag_values.reshape(-1), objective)


def power_of_two(count):
    return count & (count - 1) == 0


def whole_body(observed, blocks, diagonal, pattern):
    cols = blocks.shape[0]
    var, samp = lax.axis_size("var"), lax.axis_size("samp")
    exact = samp == 4 and samp * var == cols and var == 2 * samp and blocks.shape[2] == 128
    if exact and power_of_two(samp) and power_of_two(var):
        return column_body(observed, blocks, diagonal, pattern)
    return body(observed, blocks, diagonal, pattern)


def solution(mesh):
    placed = (P("samp", "var"), P("var", None, None, None), P("var"), P("var", None))
    return jax.shard_map(
        whole_body,
        mesh=mesh,
        in_specs=placed,
        out_specs=(P("var", None, None, None), P("var"), P()),
        check_vma=False,
    )
```

time: 84.4 us -> 76.7 us (0.909)
  Pallas kernels: 80.5 us -> 75.9 us
  other arithmetic: 2.2 us -> 0 us
    pallas_call x1, Pallas kernels: 75.2 us -> 72.4 us  [column_body(): pl.pallas_call(functools.partial(main_kernel, samp, var), out_shape=(jax....]
    pallas_call x1, Pallas kernels: 5.35 us -> 3.52 us  [column_body(): pl.pallas_call(functools.partial(unpack_kernel, samp, var, float(cols * w...]
    reduce_sum x3 -> x0, other arithmetic: 1.49 us -> none  [the longest x1 0.7 us: column_body(): off_row = jnp.sum(jnp.where(on_diag, 0, pattern), axis=1)]
where the time goes in v1:
time: 76.7 us; the launch traced here: 76.6 us
  Pallas kernels  75.9 us (99%)
    pallas_call x1, Pallas kernels, column_body(): pl.pallas_call(functools.partial(main_kernel, samp, var), out_shape=(jax....  72.4 us
    pallas_call x1, Pallas kernels, column_body(): pl.pallas_call(functools.partial(unpack_kernel, samp, var, float(cols * w...  3.52 us

profile of v1, /device:TPU:0, one launch (start us, length us, event | category | flops | bytes accessed | tf_op | source)
XLA Modules:
  0.0 76.6 jit_solution(2494812754443046930)
XLA Ops:
  0.6 72.4 %columns.1 = (bf16[4,8,2,128,128]{4,3,2,1,0:T(8,128)(2,1)S(1)}, f32[4,16,128]{2,1,0:T(8,128)S(1)}, f32[8,128]{1,0:T(8,128)S(1)}, s32[8,1,128]{2,1,0:T(1,128)S(1)}) custom-call(s32[2,32]{1,0:T(2,128)} %bitcast.4, bf16[256,4096]{1,0:T(8,128)(2,1)} %x_hbm.1, f32[32,2,128,128]{3,2,1,0:T(8,128)} %blk_hbm.1, f32[32,1,128]{2,1,0:T(1,128)} %bitcast.3), custom_call_target="tpu_custom_call" | custom-call | tf_op jit(solution)/shard_map/columns/pallas_call | solution.py:475
  73.1 3.5 %unpack.1 = (f32[32,2,128,128]{3,2,1,0:T(8,128)}, f32[32,128]{1,0:T(8,128)}, f32[2]{0:T(128)}) custom-call(s32[8,1,128]{2,1,0:T(1,128)S(1)} %get-tuple-element.10.table, bf16[4,8,2,128,128]{4,3,2,1,0:T(8,128)(2,1)S(1)} %get-tuple-element.11.fin_ref, f32[4,16,128]{2,1,0:T(8,128)S(1)} %get-tuple-element.12.tails_ref, f32[8,128]{1,0:T(8,128)S(1)} %get-tuple-element.13.whole_ref), custom_call_target="tpu_custom_call" | custom-call | tf_op jit(solution)/shard_map/unpack/pallas_call | solution.py:517

commit v2 on v1

--- a/solution.py
+++ b/solution.py
@@ -19,43 +19,50 @@
     return moved - jnp.clip(moved, -level, level)
 
 
-def flip(index, offset, count):
-    out, bit = 0, 1
-    while bit < count:
-        out = out + ((index // bit + offset // bit) % 2) * bit
-        bit *= 2
-    return out
-
-
-def inner_chip(v):
-    return ((v // 2 + 1) // 2) % 2
-
-
-def partner(v, b, k, var):
-    half = var // 2
-    close = half + 2 * inner_chip(v)
-    distant = 2 * half + 2 - close
-    high, low = k // 2, k % 2
-    return (0, 1, 2 + high, close + low, 3 - high, distant + low, distant + 1 - low, close + 1 - low)[b]
-
-
-def send_rank(i, n, samp, half):
-    if isinstance(i, int) and i < half:
-        return (n + (i - 2) * (samp // 2)) % samp
-    return 2 * n + i % 2 if n < 2 else 2 * (n - 2) + 1 - i % 2
+def mates(s):
+    return s, s + 1 - 2 * (s % 2), s + 2 - 4 * (s // 2), 3 - s
+
+
+def places(v):
+    far_half = 1 - v // 4
+    own = v // 2
+    return 2 * own, 2 * (own + 1 - 2 * (own % 2)), 2 + 2 * far_half, 6 * far_half
+
+
+OWN, NEXT, CLOSE, DISTANT = range(4)
+
+
+def batch_place(b, high, low):
+    return ((OWN, 0), (OWN, 1), (NEXT, high), (CLOSE, low), (NEXT, 1 - high),
+            (DISTANT, low), (DISTANT, 1 - low), (CLOSE, 1 - low))[b]
+
+
+def batch_owner(v, bases, b, k):
+    chip, other = batch_place(b, k // 2, k % 2)
+    return bases[chip] + (v % 2 + other) % 2
+
+
+def send_rank(chip, other, n):
+    if chip == NEXT:
+        return (n + 2 * other) % 4
+    return 2 * n + other if n < 2 else 2 * (n - 2) + 1 - other
 
 
 def main_kernel(samp, var, pat_hbm, x_hbm, blk_hbm, dia_hbm,
                 fin_ref, tails_ref, obj_ref, tab_ref,
-                pat_ref, x, blk, dia_ref, tab, ask, ask_s, far, farz, cc_out, cc_in, cc_own, cc_diag,
+                pat_ref, x, blk, dia_ref, tab, ask_s, far, farz, cc_out, cc_in, cc_own, cc_diag,
                 oo_out, oo_in, oc_own, oo_own, oo_diag, oz, acc,
-                load, tab_l, ask_ss, ask_rs, ask_l, cc_s, cc_r, z_s, z_r, oo_s, oo_r, out_s, out_r,
+                load, tab_l, ask_ss, ask_rs, cc_s, cc_r, z_s, z_r, oo_s, oo_r, out_s, out_r,
                 rel_s, rel_r, tail_s, tail_r, oz_s, oz_r):
     s = lax.axis_index("samp")
     v = lax.axis_index("var")
-    inner = inner_chip(v)
+    inner = (v // 2 + v // 4) % 2
+    core = v % 2
+    bases = places(v)
+    cores = (core, 1 - core)
+    mate = mates(s)
+    spots = [(chip, other) for chip in range(4) for other in range(2)][1:]
     rows, width = x.shape[1], x.shape[2]
-    half = var // 2
     fold_rows = width // 2
     total_rows = rows * samp
     over_first = (((0,), (0,)), ((), ()))
@@ -63,10 +70,10 @@
     cols = x.shape[0]
     bits = cols.bit_length() - 1
     barrier = pltpu.get_barrier_semaphore()
-    for i in range(1, var):
-        pl.semaphore_signal(barrier, inc=1, device_id={"var": flip(v, i, var)}, device_id_type=MESH)
+    for chip, other in spots:
+        pl.semaphore_signal(barrier, inc=1, device_id={"var": bases[chip] + cores[other]}, device_id_type=MESH)
     for d in range(1, samp):
-        pl.semaphore_signal(barrier, inc=1, device_id={"samp": flip(s, d, samp)}, device_id_type=MESH)
+        pl.semaphore_signal(barrier, inc=1, device_id={"samp": mate[d]}, device_id_type=MESH)
 
     pat_load = pltpu.make_async_copy(pat_hbm, pat_ref, load.at[cols + 1])
     pat_load.start()
@@ -109,17 +116,20 @@
             src_ref=src, dst_ref=dst, send_sem=send, recv_sem=recv,
             device_id=where, device_id_type=MESH)
 
-    def ask_copy(i):
-        u = flip(v, i, var)
-        return remote(tab_ref.at[u], ask.at[v], ask_ss.at[i], ask_rs.at[i], var=u)
-
-    def ask_load(i):
-        u = flip(v, i, var)
-        return pltpu.make_async_copy(ask.at[u], ask_s.at[u], ask_l.at[i])
-
-    def z_copy(i, k):
-        u = flip(v, i, var)
-        return remote(far.at[u, k], farz.at[v, k], z_s.at[i, k], z_r.at[i, k], var=u)
+    def place(spot):
+        return bases[spot[0]] + cores[spot[1]]
+
+    def ask_copy(u):
+        return remote(tab_ref.at[u], ask_s.at[v], ask_ss.at[u], ask_rs.at[v], var=u)
+
+    def ask_arrival(u):
+        return remote(tab_ref.at[u], ask_s.at[u], ask_ss.at[u], ask_rs.at[u], var=u)
+
+    def z_copy(u, k):
+        return remote(far.at[u, k], farz.at[v, k], z_s.at[u, k], z_r.at[v, k], var=u)
+
+    def z_arrival(u, k):
+        return remote(far.at[u, k], farz.at[u, k], z_s.at[u, k], z_r.at[u, k], var=u)
 
     def cc_copy(b, k):
         return remote(cc_out.at[b, k], cc_in.at[b, s], cc_s.at[b, k], cc_r.at[b, s], samp=k)
@@ -135,7 +145,7 @@
 
     def out_copy(d, b):
         return remote(fin_ref.at[s, b], fin_ref.at[s, b], out_s.at[d, b], out_r.at[d, b],
-                      samp=flip(s, d, samp))
+                      samp=mate[d])
 
     def near_panel(u, k):
         return x[lax.shift_right_logical(tab[u, 0, k], bits) & (cols - 1)]
@@ -171,7 +181,7 @@
 
     def start_cc(b):
         for k in range(samp):
-            u = flip(v, partner(v, b, k, var), var)
+            u = batch_owner(v, bases, b, k)
             c = near_panel(u, k)
             part = gram(c, c)
             short, diag = folded(part), diagonal_of(part)
@@ -189,7 +199,7 @@
 
     def start_oo(b, ranks, far_panel):
         for k in ranks:
-            u = flip(v, partner(v, b, k, var), var)
+            u = batch_owner(v, bases, b, k)
             o = far_panel(u, k)
             part = gram(o, jnp.concatenate([near_panel(u, k), o], axis=1))
             cross, own = part[:, :width], part[:, width:]
@@ -210,7 +220,7 @@
 
     def arrived(b, ranks):
         for k in ranks:
-            z_copy(partner(v, b, k, var), k).wait_recv()
+            z_arrival(batch_owner(v, bases, b, k), k).wait_recv()
 
     def note_sum(note):
         note = note.astype(jnp.float32)
@@ -218,12 +228,12 @@
 
     def column(b):
         for d in range(1, samp):
-            cc_arrival(b, flip(s, d, samp)).wait_recv()
-            oo_arrival(b, flip(s, d, samp)).wait_recv()
+            cc_arrival(b, mate[d]).wait_recv()
+            oo_arrival(b, mate[d]).wait_recv()
         cc, oc, oo = cc_own[b], oc_own[b], oo_own[b]
         cc_d, oo_d = cc_diag[b], oo_diag[b]
         for d in range(1, samp):
-            p = flip(s, d, samp)
+            p = mate[d]
             cc = cc + cc_in[b, p, :fold_rows].astype(jnp.float32)
             cc_d = cc_d + note_sum(cc_in[b, p, fold_rows:])
             oc = oc + oo_in[b, p, :width].astype(jnp.float32)
@@ -235,7 +245,7 @@
         high = both.astype(jnp.bfloat16)
         low = (both - high.astype(jnp.float32)).astype(jnp.bfloat16)
         gram_parts = jnp.concatenate([high, low], axis=1)
-        u = flip(v, partner(v, b, s, var), var)
+        u = batch_owner(v, bases, b, s)
         value = tab[u, 0, s]
         col = lax.shift_right_logical(value, bits) & (cols - 1)
         slot = lax.shift_right_logical(value, 2 * bits) & 1
@@ -258,16 +268,13 @@
             along = jnp.sum(jnp.where(eye, gd, 0.0), axis=0, keepdims=True)
             moved = dv - step_length * along
             dv = 0.5 * (moved + jnp.sqrt(moved * moved + 4.0 * step_length))
-        fin_ref[s, b, 0] = wd.astype(jnp.bfloat16)
-        fin_ref[s, b, 1] = wo.astype(jnp.bfloat16)
+        lead = slot == 0
+        fin_ref[s, b, 0] = jnp.where(lead, wd, wo).astype(jnp.bfloat16)
+        fin_ref[s, b, 1] = jnp.where(lead, wo, wd).astype(jnp.bfloat16)
         tails_ref[s, pl.ds(b, 1), :] = dv
 
-    def send_out(b, direct):
-        for d in range(1, samp if direct else samp - 1):
-            out_copy(d, b).start()
-
     def relay_copy(part, b):
-        near, to = flip(s, 1 + part, samp), flip(s, 2 - part, samp)
+        near, to = mate[1 + part], mate[2 - part]
         return remote(fin_ref.at[near, b, part], fin_ref.at[near, b, part],
                       rel_s.at[part, b], rel_r.at[part, b], samp=to)
 
@@ -276,11 +283,11 @@
             out_copy(1 + part, b).wait_recv()
             relay_copy(part, b).start()
 
-    close = half + 2 * inner
-    distant = 2 * half + 2 - close
-    asks = [2, 3, close, close + 1, 1, distant, distant + 1]
-    for i in asks:
-        ask_copy(i).start()
+    close = [(CLOSE, 0), (CLOSE, 1)]
+    beside = [(NEXT, 0), (NEXT, 1)]
+    distant = [(DISTANT, 0), (DISTANT, 1)]
+    for spot in close + beside + distant + [(OWN, 1)]:
+        ask_copy(place(spot)).start()
     acc[...] = jnp.zeros_like(acc)
     for x_load in x_loads:
         x_load.wait()
@@ -289,45 +296,40 @@
     tab_load.wait()
     start_cc(0)
 
-    def learn(offsets):
-        for i in offsets:
-            ask_copy(i).wait_recv()
-            ask_load(i).start()
-        for i in offsets:
-            ask_load(i).wait()
-
-    def send_panel(i, k):
-        u = flip(v, i, var)
+    def learn(wanted):
+        for spot in wanted:
+            ask_arrival(place(spot)).wait_recv()
+
+    def send_panel(spot, k):
+        u = place(spot)
         far[u, k] = x[ask_s[u, 0, k] & (cols - 1)]
-        z_copy(i, k).start()
-
-    def send_across():
-        for n in range(samp):
-            for i in (close, distant, close + 1, distant + 1):
-                send_panel(i, send_rank(i, n, samp, half))
-
-    learn([2, 3, close, close + 1])
+        z_copy(u, k).start()
+
+    def send(wanted, turns):
+        for n in turns:
+            for spot in wanted:
+                send_panel(spot, send_rank(*spot, n))
+
+    across = [close[0], distant[0], close[1], distant[1]]
 
     @pl.when(inner == 1)
     def _():
-        for i in (close, close + 1):
-            send_panel(i, send_rank(i, 0, samp, half))
-
-    for n in range(samp):
-        for i in (2, 3):
-            send_panel(i, send_rank(i, n, samp, half))
-    learn([1, distant, distant + 1])
-
-    @pl.when(inner == 1)
+        learn(close)
+        send(close, [0])
+        learn(distant + beside)
+        send(distant, [0])
+        send(beside, range(samp))
+        send(across, range(1, samp))
+
+    @pl.when(inner == 0)
     def _():
-        for i in (distant, distant + 1):
-            send_panel(i, send_rank(i, 0, samp, half))
-        for n in range(1, samp):
-            for i in (close, distant, close + 1, distant + 1):
-                send_panel(i, send_rank(i, n, samp, half))
-
+        learn(beside)
+        send(beside, range(samp))
+        learn(close + distant)
+
+    learn([(OWN, 1)])
     for k in range(samp):
-        send_panel(1, k)
+        send_panel((OWN, 1), k)
 
     every = range(samp)
     start_oo(0, every, lambda u, k: x[tab[u, 0, k] & (cols - 1)])
@@ -340,9 +342,10 @@
         arrived(b, ranks)
         start_oo(b, ranks, from_var)
 
-    def settle(b, direct=False):
+    def settle(b):
         column(b)
-        send_out(b, direct)
+        for d in range(1, samp - 1):
+            out_copy(d, b).start()
 
     last = var - 1
     take(1)
@@ -352,13 +355,13 @@
     dia_load.wait()
     settle(0)
     take(2)
-    settle(1)
     arrived(3, every)
 
     @pl.when(inner == 0)
     def _():
-        send_across()
-
+        send(across, range(samp))
+
+    settle(1)
     start_oo(3, every, from_var)
     settle(2)
     relay(0)
@@ -373,31 +376,53 @@
     relay(4)
     take(6)
     relay(5)
-    settle(6, True)
     take(last, range(samp // 2))
+    settle(6)
     take(last, range(samp // 2, samp))
+    relay(last - 1)
     column(last)
-
-    tails_ref[s, var:, :] = acc[...]
 
     def tail_copy(d):
         return remote(tails_ref.at[s], tails_ref.at[s], tail_s.at[d], tail_r.at[d],
-                      samp=flip(s, d, samp))
-
-    def oz_copy(i):
-        return remote(oz.at[v], oz.at[v], oz_s.at[i], oz_r.at[i], var=flip(v, i, var))
+                      samp=mate[d])
+
+    def oz_copy(d, u):
+        return remote(oz.at[s * var + v], oz.at[s * var + v], oz_s.at[mate[d] * var + u], oz_r.at[s * var + v],
+                      samp=mate[d], var=u)
+
+    def oz_arrival(d, u):
+        at = mate[d] * var + u
+        return remote(oz.at[at], oz.at[at], oz_s.at[at], oz_r.at[at], samp=mate[d], var=u)
+
+    halves = [acc[step:step + 1, :] + pltpu.roll(acc[step:step + 1, :], fold_rows, 1) for step in range(STEPS)]
+    oz[s * var + v] = jnp.where(fold_col[:1] < fold_rows, halves[0], halves[1])
+    peers = [(d, place(spot)) for d in range(samp - 1, -1, -1) for spot in spots[::-1] + [(OWN, 0)]][:-1]
+    for peer in peers:
+        oz_copy(*peer).start()
+    for d in range(1, samp - 1):
+        out_copy(d, last).start()
+
+    early_owner = s < samp // 2
+    late_owner = s >= samp // 2
+
+    @pl.when(late_owner)
+    def _():
+        out_copy(samp - 1, last).start()
 
     for d in range(1, samp):
         tail_copy(d).start()
-    send_out(last, True)
-    for d in range(1, samp):
-        tail_copy(d).wait_recv()
-    group = tails_ref[0, var:, :]
-    for k in range(1, samp):
-        group = group + tails_ref[k, var:, :]
-    oz[v] = group
-    for i in range(1, var):
-        oz_copy(i).start()
+
+    @pl.when(early_owner)
+    def _():
+        out_copy(1, last).wait_recv()
+        relay_copy(0, last).start()
+        out_copy(2, last).wait_recv()
+
+    @pl.when(late_owner)
+    def _():
+        out_copy(2, last).wait_recv()
+        relay_copy(1, last).start()
+        out_copy(1, last).wait_recv()
 
     def finish(b, carry):
         for d in range(1, samp - 1):
@@ -419,45 +444,72 @@
                 return carry
 
             lax.fori_loop(0, var, sent, 0)
-    lax.fori_loop(0, var - 2, finish_relay, 0)
-    for b in range(var - 2, var):
-        for d in range(1, samp - 1):
-            out_copy(d, b).wait_recv()
-        out_copy(samp - 1, b).wait()
+    lax.fori_loop(0, last, finish_relay, 0)
+
+    @pl.when(early_owner)
+    def _():
+        relay_copy(0, last).wait_send()
+        out_copy(samp - 1, last).wait_recv()
+
+    @pl.when(late_owner)
+    def _():
+        relay_copy(1, last).wait_send()
+        out_copy(samp - 1, last).wait_send()
+        for part in range(2):
+            relay_copy(part, last).wait_recv()
+
     for d in range(1, samp):
-        tail_copy(d).wait_send()
-    for i in range(1, var):
-        ask_copy(i).wait_send()
+        tail_copy(d).wait()
+    for spot in spots:
+        ask_copy(place(spot)).wait_send()
         for k in range(samp):
-            z_copy(i, k).wait_send()
-    for i in range(1, var):
-        oz_copy(i).wait()
+            z_copy(place(spot), k).wait_send()
+    for peer in peers:
+        oz_copy(*peer).wait_send()
+        oz_arrival(*peer).wait_recv()
     whole = oz[0]
-    for u in range(1, var):
-        whole = whole + oz[u]
+    for e in range(1, samp * var):
+        whole = whole + oz[e]
     obj_ref[...] = whole
 
 
-def unpack_kernel(samp, var, order, bits, table, fin_ref, tails_ref, whole_ref,
-                  out_hbm, dia_ref, obj_ref, stage, sem):
+def unpack_kernel(samp, var, order, bits, tab, fin_ref, tails_ref, whole_ref,
+                  out_hbm, dia_hbm, obj_hbm, table, stage, dia, obj, sem, extra):
     v = lax.axis_index("var")
-    last = (1 << bits) - 1
-    copies = []
+    cols, width = dia.shape
+    load = pltpu.make_async_copy(tab, table, extra.at[0])
+    load.start()
+    lane = lax.broadcasted_iota(jnp.int32, (1, width), 1)
+    part = lane // (width // 2)
+    for step in range(STEPS):
+        obj[step] = jnp.sum(jnp.where(part == step, whole_ref[...], 0.0)) / order
+    rest = [pltpu.make_async_copy(obj, obj_hbm, extra.at[1]), pltpu.make_async_copy(dia, dia_hbm, extra.at[2])]
+    rest[0].start()
+
+    bases = places(v)
+
+    def place(b, k):
+        return lax.shift_right_logical(table[batch_owner(v, bases, b, k), 0, k], bits) & (cols - 1)
+
+    def copy(b, k):
+        return pltpu.make_async_copy(stage.at[b, k], out_hbm.at[place(b, k)], sem.at[b, k])
+
     for b in range(var):
         for k in range(samp):
-            value = table[flip(v, partner(v, b, k, var), var), 0, k]
-            col = lax.shift_right_logical(value, bits) & last
-            slot = lax.shift_right_logical(value, 2 * bits) & 1
-            stage[b, k, slot] = fin_ref[k, b, 0].astype(jnp.float32)
-            stage[b, k, 1 - slot] = fin_ref[k, b, 1].astype(jnp.float32)
-            copy = pltpu.make_async_copy(stage.at[b, k], out_hbm.at[col], sem.at[b, k])
-            copy.start()
-            copies.append(copy)
-            dia_ref[pl.ds(col, 1), :] = tails_ref[k, b:b + 1, :]
-    for step in range(STEPS):
-        obj_ref[step] = jnp.sum(whole_ref[step:step + 1, :]) / order
-    for copy in copies:
-        copy.wait()
+            stage[b, k] = fin_ref[k, b].astype(jnp.float32)
+    load.wait()
+    for b in range(var):
+        for k in range(samp):
+            copy(b, k).start()
+    for b in range(var):
+        for k in range(samp):
+            dia[pl.ds(place(b, k), 1), :] = tails_ref[k, b:b + 1, :]
+    rest[1].start()
+    for b in range(var):
+        for k in range(samp):
+            pltpu.make_async_copy(stage.at[b, k], out_hbm.at[0], sem.at[b, k]).wait()
+    for other in rest:
+        other.wait()
 
 
 def column_body(observed, blocks, diagonal, pattern):
@@ -476,8 +528,8 @@
         functools.partial(main_kernel, samp, var),
         out_shape=(
             jax.ShapeDtypeStruct((samp, var, 2, width, width), bf16),
-            jax.ShapeDtypeStruct((samp, var + 8, width), f32),
-            jax.ShapeDtypeStruct((8, width), f32),
+            jax.ShapeDtypeStruct((samp, var, width), f32),
+            jax.ShapeDtypeStruct((1, width), f32),
             jax.ShapeDtypeStruct((var, 1, width), jnp.int32),
         ),
         in_specs=[hbm] * 4,
@@ -488,7 +540,6 @@
             pltpu.VMEM(blocks.shape, f32),
             pltpu.VMEM((cols, 1, width), f32),
             pltpu.SMEM((var, 1, width), jnp.int32),
-            pltpu.VMEM((var, 1, width), jnp.int32),
             pltpu.SMEM((var, 1, width), jnp.int32),
             pltpu.VMEM((var, samp, rows, width), observed.dtype),
             pltpu.VMEM((var, samp, rows, width), observed.dtype),
@@ -501,12 +552,13 @@
             pltpu.VMEM((var, width, width), f32),
             pltpu.VMEM((var, width // 2, width), f32),
             pltpu.VMEM((var, 1, width), f32),
-            pltpu.VMEM((var, 8, width), f32),
+            pltpu.VMEM((samp * var, 1, width), f32),
             pltpu.VMEM((8, width), f32),
-            dma((cols + 3,)), dma, dma((var,)), dma((var,)), dma((var,)),
+            dma((cols + 3,)), dma, dma((var,)), dma((var,)),
             dma((var, samp)), dma((var, samp)), dma((var, samp)), dma((var, samp)),
             dma((var, samp)), dma((var, samp)), dma((samp, var)), dma((samp, var)),
-            dma((2, var)), dma((2, var)), dma((samp,)), dma((samp,)), dma((var,)), dma((var,)),
+            dma((2, var)), dma((2, var)), dma((samp,)), dma((samp,)),
+            dma((samp * var,)), dma((samp * var,)),
         ],
         compiler_params=pltpu.CompilerParams(
             collective_id=0, has_side_effects=True, vmem_limit_bytes=40 * 2 ** 20),
@@ -521,11 +573,14 @@
             jax.ShapeDtypeStruct((cols, width), f32),
             jax.ShapeDtypeStruct((STEPS,), f32),
         ),
-        in_specs=[smem, vmem, vmem, vmem],
-        out_specs=(hbm, vmem, smem),
+        in_specs=[vmem] * 4,
+        out_specs=(hbm,) * 3,
         scratch_shapes=[
+            pltpu.SMEM((var, 1, width), jnp.int32),
             pltpu.VMEM((var, samp, 2, width, width), f32),
-            dma((var, samp)),
+            pltpu.VMEM((cols, width), f32),
+            pltpu.SMEM((STEPS,), f32),
+            dma((var, samp)), dma((3,)),
         ],
         compiler_params=pltpu.CompilerParams(vmem_limit_bytes=16 * 2 ** 20),
         name="unpack",

time: 76.7 us -> 73.8 us (0.962)
  Pallas kernels: 75.9 us -> 73 us
    pallas_call x1, Pallas kernels: 72.4 us -> 70.1 us  [column_body(): pl.pallas_call(functools.partial(main_kernel, samp, var), out_shape=(jax....]
where the time goes in v2:
time: 73.8 us; the launch traced here: 73.7 us
  Pallas kernels  73 us (99%)
    pallas_call x1, Pallas kernels, column_body(): pl.pallas_call(functools.partial(main_kernel, samp, var), out_shape=(jax....  70.1 us
    pallas_call x1, Pallas kernels, column_body(): pl.pallas_call(functools.partial(unpack_kernel, samp, var, float(cols * w...  2.94 us

profile of v2, /device:TPU:0, one launch (start us, length us, event | category | flops | bytes accessed | tf_op | source)
XLA Modules:
  0.0 73.7 jit_solution(17005496583826413652)
XLA Ops:
  0.6 70.1 %columns.1 = (bf16[4,8,2,128,128]{4,3,2,1,0:T(8,128)(2,1)S(1)}, f32[4,8,128]{2,1,0:T(8,128)S(1)}, f32[1,128]{1,0:T(1,128)S(1)}, s32[8,1,128]{2,1,0:T(1,128)S(1)}) custom-call(s32[2,32]{1,0:T(2,128)} %bitcast.4, bf16[256,4096]{1,0:T(8,128)(2,1)} %x_hbm.1, f32[32,2,128,128]{3,2,1,0:T(8,128)} %blk_hbm.1, f32[32,1,128]{2,1,0:T(1,128)} %bitcast.3), custom_call_target="tpu_custom_call" | custom-call | tf_op jit(solution)/shard_map/columns/pallas_call | solution.py:527
  70.7 2.9 %unpack.1 = (f32[32,2,128,128]{3,2,1,0:T(8,128)}, f32[32,128]{1,0:T(8,128)}, f32[2]{0:T(128)}) custom-call(s32[8,1,128]{2,1,0:T(1,128)S(1)} %get-tuple-element.10.tab, bf16[4,8,2,128,128]{4,3,2,1,0:T(8,128)(2,1)S(1)} %get-tuple-element.11.fin_ref, f32[4,8,128]{2,1,0:T(8,128)S(1)} %get-tuple-element.12.tails_ref, f32[1,128]{1,0:T(1,128)S(1)} %get-tuple-element.13.whole_ref), custom_call_target="tpu_custom_call" | custom-call | tf_op jit(solution)/shard_map/unpack/pallas_call | solution.py:569

commit v3 on v2

--- a/solution.py
+++ b/solution.py
@@ -75,16 +75,16 @@
     for d in range(1, samp):
         pl.semaphore_signal(barrier, inc=1, device_id={"samp": mate[d]}, device_id_type=MESH)
 
-    pat_load = pltpu.make_async_copy(pat_hbm, pat_ref, load.at[cols + 1])
+    pat_load = pltpu.make_async_copy(pat_hbm, pat_ref, load.at[1])
     pat_load.start()
     x_loads = [
-        pltpu.make_async_copy(x_hbm.at[:, l * width:(l + 1) * width], x.at[l], load.at[l])
+        pltpu.make_async_copy(x_hbm.at[:, l * width:(l + 1) * width], x.at[l], load.at[0])
         for l in range(cols)
     ]
     for x_load in x_loads:
         x_load.start()
-    blk_load = pltpu.make_async_copy(blk_hbm, blk, load.at[cols])
-    dia_load = pltpu.make_async_copy(dia_hbm, dia_ref, load.at[cols + 2])
+    blk_load = pltpu.make_async_copy(blk_hbm, blk, load.at[2])
+    dia_load = pltpu.make_async_copy(dia_hbm, dia_ref, load.at[3])
 
     pat_load.wait()
     first, second = pat_ref[0:1, :], pat_ref[1:2, :]
@@ -120,32 +120,27 @@
         return bases[spot[0]] + cores[spot[1]]
 
     def ask_copy(u):
-        return remote(tab_ref.at[u], ask_s.at[v], ask_ss.at[u], ask_rs.at[v], var=u)
+        return remote(tab_ref.at[u], ask_s.at[v], ask_ss, ask_rs.at[v], var=u)
 
     def ask_arrival(u):
-        return remote(tab_ref.at[u], ask_s.at[u], ask_ss.at[u], ask_rs.at[u], var=u)
-
-    def z_copy(u, k):
-        return remote(far.at[u, k], farz.at[v, k], z_s.at[u, k], z_r.at[v, k], var=u)
-
-    def z_arrival(u, k):
-        return remote(far.at[u, k], farz.at[u, k], z_s.at[u, k], z_r.at[u, k], var=u)
+        return remote(tab_ref.at[u], ask_s.at[u], ask_ss, ask_rs.at[u], var=u)
+
+    def z_copy(u, k, turn):
+        return remote(far.at[u, k], farz.at[v, k], z_s, z_r.at[turn], var=u)
 
     def cc_copy(b, k):
-        return remote(cc_out.at[b, k], cc_in.at[b, s], cc_s.at[b, k], cc_r.at[b, s], samp=k)
+        return remote(cc_out.at[b, k], cc_in.at[b, s], cc_s, cc_r.at[b], samp=k)
 
     def oo_copy(b, k):
-        return remote(oo_out.at[b, k], oo_in.at[b, s], oo_s.at[b, k], oo_r.at[b, s], samp=k)
-
-    def cc_arrival(b, k):
-        return remote(cc_out.at[b, k], cc_in.at[b, k], cc_s.at[b, k], cc_r.at[b, k], samp=k)
-
-    def oo_arrival(b, k):
-        return remote(oo_out.at[b, k], oo_in.at[b, k], oo_s.at[b, k], oo_r.at[b, k], samp=k)
+        return remote(oo_out.at[b, k], oo_in.at[b, s], oo_s, oo_r.at[b], samp=k)
 
     def out_copy(d, b):
-        return remote(fin_ref.at[s, b], fin_ref.at[s, b], out_s.at[d, b], out_r.at[d, b],
+        direct = d == samp - 1
+        return remote(fin_ref.at[s, b], fin_ref.at[s, b], out_s.at[int(direct)], out_r.at[var if direct else b],
                       samp=mate[d])
+
+    def together(array, send, recv):
+        return remote(array, array, send, recv, samp=mate[1])
 
     def near_panel(u, k):
         return x[lax.shift_right_logical(tab[u, 0, k], bits) & (cols - 1)]
@@ -218,18 +213,16 @@
             def _():
                 oo_copy(b, k).start()
 
-    def arrived(b, ranks):
-        for k in ranks:
-            z_arrival(batch_owner(v, bases, b, k), k).wait_recv()
+    def arrived(turn, ranks):
+        together(farz.at[0, :len(ranks)], z_s, z_r.at[turn]).wait_recv()
 
     def note_sum(note):
         note = note.astype(jnp.float32)
         return note[0:1] + note[1:2]
 
     def column(b):
-        for d in range(1, samp):
-            cc_arrival(b, mate[d]).wait_recv()
-            oo_arrival(b, mate[d]).wait_recv()
+        together(cc_in.at[b, :samp - 1], cc_s, cc_r.at[b]).wait_recv()
+        together(oo_in.at[b, :samp - 1], oo_s, oo_r.at[b]).wait_recv()
         cc, oc, oo = cc_own[b], oc_own[b], oo_own[b]
         cc_d, oo_d = cc_diag[b], oo_diag[b]
         for d in range(1, samp):
@@ -273,14 +266,17 @@
         fin_ref[s, b, 1] = jnp.where(lead, wo, wd).astype(jnp.bfloat16)
         tails_ref[s, pl.ds(b, 1), :] = dv
 
-    def relay_copy(part, b):
+    def relay_copy(part, b, final=0):
         near, to = mate[1 + part], mate[2 - part]
         return remote(fin_ref.at[near, b, part], fin_ref.at[near, b, part],
-                      rel_s.at[part, b], rel_r.at[part, b], samp=to)
+                      rel_s.at[final], rel_r.at[final], samp=to)
+
+    def beside_done(b):
+        together(fin_ref.at[0, :samp - 2], out_s.at[0], out_r.at[b]).wait_recv()
 
     def relay(b):
+        beside_done(b)
         for part in range(2):
-            out_copy(1 + part, b).wait_recv()
             relay_copy(part, b).start()
 
     close = [(CLOSE, 0), (CLOSE, 1)]
@@ -289,8 +285,7 @@
     for spot in close + beside + distant + [(OWN, 1)]:
         ask_copy(place(spot)).start()
     acc[...] = jnp.zeros_like(acc)
-    for x_load in x_loads:
-        x_load.wait()
+    pltpu.make_async_copy(x, x, load.at[0]).wait()
     blk_load.start()
     dia_load.start()
     tab_load.wait()
@@ -300,36 +295,38 @@
         for spot in wanted:
             ask_arrival(place(spot)).wait_recv()
 
-    def send_panel(spot, k):
+    def send_panel(spot, k, turn):
         u = place(spot)
         far[u, k] = x[ask_s[u, 0, k] & (cols - 1)]
-        z_copy(u, k).start()
-
-    def send(wanted, turns):
+        z_copy(u, k, turn).start()
+
+    def send(wanted, turns, at):
         for n in turns:
             for spot in wanted:
-                send_panel(spot, send_rank(*spot, n))
+                send_panel(spot, send_rank(*spot, n), at[n])
+
+    near_turns, inner_turns, outer_turns = (2, 2, 4, 4), (3, 3, 7, 0), (5, 5, 6, 6)
 
     across = [close[0], distant[0], close[1], distant[1]]
 
     @pl.when(inner == 1)
     def _():
         learn(close)
-        send(close, [0])
+        send(close, [0], inner_turns)
         learn(distant + beside)
-        send(distant, [0])
-        send(beside, range(samp))
-        send(across, range(1, samp))
+        send(distant, [0], inner_turns)
+        send(beside, range(samp), near_turns)
+        send(across, range(1, samp), inner_turns)
 
     @pl.when(inner == 0)
     def _():
         learn(beside)
-        send(beside, range(samp))
+        send(beside, range(samp), near_turns)
         learn(close + distant)
 
     learn([(OWN, 1)])
     for k in range(samp):
-        send_panel((OWN, 1), k)
+        send_panel((OWN, 1), k, 1)
 
     every = range(samp)
     start_oo(0, every, lambda u, k: x[tab[u, 0, k] & (cols - 1)])
@@ -338,8 +335,8 @@
     def from_var(u, k):
         return farz[u, k]
 
-    def take(b, ranks=every):
-        arrived(b, ranks)
+    def take(b, ranks=every, turn=None):
+        arrived(b if turn is None else turn, ranks)
         start_oo(b, ranks, from_var)
 
     def settle(b):
@@ -359,7 +356,7 @@
 
     @pl.when(inner == 0)
     def _():
-        send(across, range(samp))
+        send(across, range(samp), outer_turns)
 
     settle(1)
     start_oo(3, every, from_var)
@@ -378,21 +375,17 @@
     relay(5)
     take(last, range(samp // 2))
     settle(6)
-    take(last, range(samp // 2, samp))
+    take(last, range(samp // 2, samp), 0)
     relay(last - 1)
     column(last)
 
     def tail_copy(d):
-        return remote(tails_ref.at[s], tails_ref.at[s], tail_s.at[d], tail_r.at[d],
+        return remote(tails_ref.at[s], tails_ref.at[s], tail_s, tail_r,
                       samp=mate[d])
 
     def oz_copy(d, u):
-        return remote(oz.at[s * var + v], oz.at[s * var + v], oz_s.at[mate[d] * var + u], oz_r.at[s * var + v],
+        return remote(oz.at[s * var + v], oz.at[s * var + v], oz_s, oz_r,
                       samp=mate[d], var=u)
-
-    def oz_arrival(d, u):
-        at = mate[d] * var + u
-        return remote(oz.at[at], oz.at[at], oz_s.at[at], oz_r.at[at], samp=mate[d], var=u)
 
     halves = [acc[step:step + 1, :] + pltpu.roll(acc[step:step + 1, :], fold_rows, 1) for step in range(STEPS)]
     oz[s * var + v] = jnp.where(fold_col[:1] < fold_rows, halves[0], halves[1])
@@ -412,61 +405,36 @@
     for d in range(1, samp):
         tail_copy(d).start()
 
+    beside_done(last)
+
     @pl.when(early_owner)
     def _():
-        out_copy(1, last).wait_recv()
-        relay_copy(0, last).start()
-        out_copy(2, last).wait_recv()
+        relay_copy(0, last, 1).start()
 
     @pl.when(late_owner)
     def _():
-        out_copy(2, last).wait_recv()
-        relay_copy(1, last).start()
-        out_copy(1, last).wait_recv()
-
-    def finish(b, carry):
-        for d in range(1, samp - 1):
-            out_copy(d, b).wait_send()
-        return carry
-
-    def finish_relay(b, carry):
-        for part in range(2):
-            relay_copy(part, b).wait()
-        return carry
-
-    lax.fori_loop(0, var, finish, 0)
-    for k in range(samp):
-        @pl.when(s != k)
-        def _():
-            def sent(b, carry):
-                cc_copy(b, k).wait_send()
-                oo_copy(b, k).wait_send()
-                return carry
-
-            lax.fori_loop(0, var, sent, 0)
-    lax.fori_loop(0, last, finish_relay, 0)
+        relay_copy(1, last, 1).start()
+
+    sent = var * (samp - 1) // samp
+    together(cc_out.at[:sent], cc_s, cc_r.at[0]).wait_send()
+    together(oo_out.at[:sent], oo_s, oo_r.at[0]).wait_send()
+    together(fin_ref.at[:samp - 2], out_s.at[0], out_r.at[0]).wait_send()
+    together(fin_ref.at[0, :last], rel_s.at[0], rel_r.at[0]).wait()
+    together(fin_ref.at[0, 0, 0], rel_s.at[1], rel_r.at[1]).wait_send()
 
     @pl.when(early_owner)
     def _():
-        relay_copy(0, last).wait_send()
-        out_copy(samp - 1, last).wait_recv()
+        together(fin_ref.at[0, 0], out_s.at[1], out_r.at[var]).wait_recv()
 
     @pl.when(late_owner)
     def _():
-        relay_copy(1, last).wait_send()
-        out_copy(samp - 1, last).wait_send()
-        for part in range(2):
-            relay_copy(part, last).wait_recv()
-
-    for d in range(1, samp):
-        tail_copy(d).wait()
-    for spot in spots:
-        ask_copy(place(spot)).wait_send()
-        for k in range(samp):
-            z_copy(place(spot), k).wait_send()
-    for peer in peers:
-        oz_copy(*peer).wait_send()
-        oz_arrival(*peer).wait_recv()
+        together(fin_ref.at[0, 0], out_s.at[1], out_r.at[var]).wait_send()
+        together(fin_ref.at[0, 0], rel_s.at[1], rel_r.at[1]).wait_recv()
+
+    together(tails_ref.at[:samp - 1], tail_s, tail_r).wait()
+    together(tab_ref.at[:var - 1], ask_ss, ask_rs.at[0]).wait_send()
+    together(far.at[:var - 1], z_s, z_r.at[0]).wait_send()
+    together(oz.at[:samp * var - 1], oz_s, oz_r).wait()
     whole = oz[0]
     for e in range(1, samp * var):
         whole = whole + oz[e]
@@ -474,7 +442,7 @@
 
 
 def unpack_kernel(samp, var, order, bits, tab, fin_ref, tails_ref, whole_ref,
-                  out_hbm, dia_hbm, obj_hbm, table, stage, dia, obj, sem, extra):
+                  out_hbm, dia_hbm, obj_hbm, table, stage, dia, obj, extra):
     v = lax.axis_index("var")
     cols, width = dia.shape
     load = pltpu.make_async_copy(tab, table, extra.at[0])
@@ -492,11 +460,11 @@
         return lax.shift_right_logical(table[batch_owner(v, bases, b, k), 0, k], bits) & (cols - 1)
 
     def copy(b, k):
-        return pltpu.make_async_copy(stage.at[b, k], out_hbm.at[place(b, k)], sem.at[b, k])
+        return pltpu.make_async_copy(stage.at[b * samp + k], out_hbm.at[place(b, k)], extra.at[3])
 
     for b in range(var):
         for k in range(samp):
-            stage[b, k] = fin_ref[k, b].astype(jnp.float32)
+            stage[b * samp + k] = fin_ref[k, b].astype(jnp.float32)
     load.wait()
     for b in range(var):
         for k in range(samp):
@@ -505,9 +473,7 @@
         for k in range(samp):
             dia[pl.ds(place(b, k), 1), :] = tails_ref[k, b:b + 1, :]
     rest[1].start()
-    for b in range(var):
-        for k in range(samp):
-            pltpu.make_async_copy(stage.at[b, k], out_hbm.at[0], sem.at[b, k]).wait()
+    pltpu.make_async_copy(stage, out_hbm, extra.at[3]).wait()
     for other in rest:
         other.wait()
 
@@ -554,11 +520,8 @@
             pltpu.VMEM((var, 1, width), f32),
             pltpu.VMEM((samp * var, 1, width), f32),
             pltpu.VMEM((8, width), f32),
-            dma((cols + 3,)), dma, dma((var,)), dma((var,)),
-            dma((var, samp)), dma((var, samp)), dma((var, samp)), dma((var, samp)),
-            dma((var, samp)), dma((var, samp)), dma((samp, var)), dma((samp, var)),
-            dma((2, var)), dma((2, var)), dma((samp,)), dma((samp,)),
-            dma((samp * var,)), dma((samp * var,)),
+            dma((4,)), dma, dma, dma((var,)), dma, dma((var,)), dma, dma((var,)), dma, dma((var,)),
+            dma((2,)), dma((var + 1,)), dma((2,)), dma((2,)), dma, dma, dma, dma,
         ],
         compiler_params=pltpu.CompilerParams(
             collective_id=0, has_side_effects=True, vmem_limit_bytes=40 * 2 ** 20),
@@ -577,10 +540,10 @@
         out_specs=(hbm,) * 3,
         scratch_shapes=[
             pltpu.SMEM((var, 1, width), jnp.int32),
-            pltpu.VMEM((var, samp, 2, width, width), f32),
+            pltpu.VMEM((cols, 2, width, width), f32),
             pltpu.VMEM((cols, width), f32),
             pltpu.SMEM((STEPS,), f32),
-            dma((var, samp)), dma((3,)),
+            dma((4,)),
         ],
         compiler_params=pltpu.CompilerParams(vmem_limit_bytes=16 * 2 ** 20),
         name="unpack",

time: 73.8 us -> 70.3 us (0.953)
  Pallas kernels: 73 us -> 69.5 us
    pallas_call x1, Pallas kernels: 70.1 us -> 66.8 us  [column_body(): pl.pallas_call(functools.partial(main_kernel, samp, var), out_shape=(jax....]
where the time goes in v3:
time: 70.3 us; the launch traced here: 70.1 us
  Pallas kernels  69.5 us (99%)
    pallas_call x1, Pallas kernels, column_body(): pl.pallas_call(functools.partial(main_kernel, samp, var), out_shape=(jax....  66.8 us
    pallas_call x1, Pallas kernels, column_body(): pl.pallas_call(functools.partial(unpack_kernel, samp, var, float(cols * w...  2.65 us

profile of v3, /device:TPU:0, one launch (start us, length us, event | category | flops | bytes accessed | tf_op | source)
XLA Modules:
  0.0 70.1 jit_solution(14404957932232980089)
XLA Ops:
  0.6 66.8 %columns.1 = (bf16[4,8,2,128,128]{4,3,2,1,0:T(8,128)(2,1)S(1)}, f32[4,8,128]{2,1,0:T(8,128)S(1)}, f32[1,128]{1,0:T(1,128)S(1)}, s32[8,1,128]{2,1,0:T(1,128)S(1)}) custom-call(s32[2,32]{1,0:T(2,128)} %bitcast.4, bf16[256,4096]{1,0:T(8,128)(2,1)} %x_hbm.1, f32[32,2,128,128]{3,2,1,0:T(8,128)} %blk_hbm.1, f32[32,1,128]{2,1,0:T(1,128)} %bitcast.3), custom_call_target="tpu_custom_call" | custom-call | tf_op jit(solution)/shard_map/columns/pallas_call | solution.py:493
  67.5 2.6 %unpack.1 = (f32[32,2,128,128]{3,2,1,0:T(8,128)}, f32[32,128]{1,0:T(8,128)}, f32[2]{0:T(128)}) custom-call(s32[8,1,128]{2,1,0:T(1,128)S(1)} %get-tuple-element.10.tab, bf16[4,8,2,128,128]{4,3,2,1,0:T(8,128)(2,1)S(1)} %get-tuple-element.11.fin_ref, f32[4,8,128]{2,1,0:T(8,128)S(1)} %get-tuple-element.12.tails_ref, f32[1,128]{1,0:T(1,128)S(1)} %get-tuple-element.13.whole_ref), custom_call_target="tpu_custom_call" | custom-call | tf_op jit(solution)/shard_map/unpack/pallas_call | solution.py:532

commit v4 on v3

--- a/solution.py
+++ b/solution.py
@@ -307,6 +307,14 @@
 
     near_turns, inner_turns, outer_turns = (2, 2, 4, 4), (3, 3, 7, 0), (5, 5, 6, 6)
 
+    def send_last():
+        for n, to, chip in [(n, to, chip) for to in range(2) for n in (2, 3) for chip in (CLOSE, DISTANT)]:
+            other = (core + to) % 2
+            k = 2 * (n - 2) + 1 - other
+            u = bases[chip] + to
+            far[u, k] = x[ask_s[u, 0, k] & (cols - 1)]
+            z_copy(u, k, inner_turns[n]).start()
+
     across = [close[0], distant[0], close[1], distant[1]]
 
     @pl.when(inner == 1)
@@ -316,7 +324,8 @@
         learn(distant + beside)
         send(distant, [0], inner_turns)
         send(beside, range(samp), near_turns)
-        send(across, range(1, samp), inner_turns)
+        send(across, [1], inner_turns)
+        send_last()
 
     @pl.when(inner == 0)
     def _():
@@ -374,9 +383,17 @@
     take(6)
     relay(5)
     take(last, range(samp // 2))
-    settle(6)
+
+    @pl.when(core == 1)
+    def _():
+        settle(last - 1)
+
     take(last, range(samp // 2, samp), 0)
-    relay(last - 1)
+
+    @pl.when(core == 0)
+    def _():
+        settle(last - 1)
+
     column(last)
 
     def tail_copy(d):
@@ -404,6 +421,7 @@
 
     for d in range(1, samp):
         tail_copy(d).start()
+    relay(last - 1)
 
     beside_done(last)
 

time: 70.3 us -> 67.6 us (0.962)
  Pallas kernels: 69.5 us -> 66.4 us
    pallas_call x1, Pallas kernels: 66.8 us -> 63.7 us  [column_body(): pl.pallas_call(functools.partial(main_kernel, samp, var), out_shape=(jax....]
where the time goes in v4:
time: 67.6 us; the launch traced here: 67 us
  Pallas kernels  66.4 us (98%)
    pallas_call x1, Pallas kernels, column_body(): pl.pallas_call(functools.partial(main_kernel, samp, var), out_shape=(jax....  63.7 us
    pallas_call x1, Pallas kernels, column_body(): pl.pallas_call(functools.partial(unpack_kernel, samp, var, float(cols * w...  2.65 us

profile of v4, /device:TPU:0, one launch (start us, length us, event | category | flops | bytes accessed | tf_op | source)
XLA Modules:
  0.0 67.0 jit_solution(10224344157735952384)
XLA Ops:
  0.6 63.7 %columns.1 = (bf16[4,8,2,128,128]{4,3,2,1,0:T(8,128)(2,1)S(1)}, f32[4,8,128]{2,1,0:T(8,128)S(1)}, f32[1,128]{1,0:T(1,128)S(1)}, s32[8,1,128]{2,1,0:T(1,128)S(1)}) custom-call(s32[2,32]{1,0:T(2,128)} %bitcast.4, bf16[256,4096]{1,0:T(8,128)(2,1)} %x_hbm.1, f32[32,2,128,128]{3,2,1,0:T(8,128)} %blk_hbm.1, f32[32,1,128]{2,1,0:T(1,128)} %bitcast.3), custom_call_target="tpu_custom_call" | custom-call | tf_op jit(solution)/shard_map/columns/pallas_call | solution.py:511
  64.4 2.6 %unpack.1 = (f32[32,2,128,128]{3,2,1,0:T(8,128)}, f32[32,128]{1,0:T(8,128)}, f32[2]{0:T(128)}) custom-call(s32[8,1,128]{2,1,0:T(1,128)S(1)} %get-tuple-element.10.tab, bf16[4,8,2,128,128]{4,3,2,1,0:T(8,128)(2,1)S(1)} %get-tuple-element.11.fin_ref, f32[4,8,128]{2,1,0:T(8,128)S(1)} %get-tuple-element.12.tails_ref, f32[1,128]{1,0:T(1,128)S(1)} %get-tuple-element.13.whole_ref), custom_call_target="tpu_custom_call" | custom-call | tf_op jit(solution)/shard_map/unpack/pallas_call | solution.py:550

commit v5 on v3

--- a/solution.py
+++ b/solution.py
@@ -307,6 +307,16 @@
 
     near_turns, inner_turns, outer_turns = (2, 2, 4, 4), (3, 3, 7, 0), (5, 5, 6, 6)
 
+    def send_by_core(turns, at):
+        for to in range(2):
+            for n in turns:
+                for chip in (CLOSE, DISTANT):
+                    other = (core + to) % 2
+                    k = 2 * n + other if n < 2 else 2 * (n - 2) + 1 - other
+                    u = bases[chip] + to
+                    far[u, k] = x[ask_s[u, 0, k] & (cols - 1)]
+                    z_copy(u, k, at[n]).start()
+
     across = [close[0], distant[0], close[1], distant[1]]
 
     @pl.when(inner == 1)
@@ -316,7 +326,8 @@
         learn(distant + beside)
         send(distant, [0], inner_turns)
         send(beside, range(samp), near_turns)
-        send(across, range(1, samp), inner_turns)
+        send(across, [1], inner_turns)
+        send_by_core((2, 3), inner_turns)
 
     @pl.when(inner == 0)
     def _():
@@ -356,7 +367,8 @@
 
     @pl.when(inner == 0)
     def _():
-        send(across, range(samp), outer_turns)
+        send(across, range(2), outer_turns)
+        send_by_core((2, 3), outer_turns)
 
     settle(1)
     start_oo(3, every, from_var)
@@ -373,10 +385,9 @@
     relay(4)
     take(6)
     relay(5)
+    settle(last - 1)
     take(last, range(samp // 2))
-    settle(6)
     take(last, range(samp // 2, samp), 0)
-    relay(last - 1)
     column(last)
 
     def tail_copy(d):
@@ -404,6 +415,7 @@
 
     for d in range(1, samp):
         tail_copy(d).start()
+    relay(last - 1)
 
     beside_done(last)
 

time: 70.3 us -> 66.6 us (0.947)
  Pallas kernels: 69.5 us -> 65.6 us
    pallas_call x1, Pallas kernels: 66.8 us -> 63 us  [column_body(): pl.pallas_call(functools.partial(main_kernel, samp, var), out_shape=(jax....]
where the time goes in v5:
time: 66.6 us; the launch traced here: 66.3 us
  Pallas kernels  65.6 us (98%)
    pallas_call x1, Pallas kernels, column_body(): pl.pallas_call(functools.partial(main_kernel, samp, var), out_shape=(jax....  63 us
    pallas_call x1, Pallas kernels, column_body(): pl.pallas_call(functools.partial(unpack_kernel, samp, var, float(cols * w...  2.65 us

profile of v5, /device:TPU:0, one launch (start us, length us, event | category | flops | bytes accessed | tf_op | source)
XLA Modules:
  0.0 66.3 jit_solution(13322899122857176781)
XLA Ops:
  0.6 63.0 %columns.1 = (bf16[4,8,2,128,128]{4,3,2,1,0:T(8,128)(2,1)S(1)}, f32[4,8,128]{2,1,0:T(8,128)S(1)}, f32[1,128]{1,0:T(1,128)S(1)}, s32[8,1,128]{2,1,0:T(1,128)S(1)}) custom-call(s32[2,32]{1,0:T(2,128)} %bitcast.4, bf16[256,4096]{1,0:T(8,128)(2,1)} %x_hbm.1, f32[32,2,128,128]{3,2,1,0:T(8,128)} %blk_hbm.1, f32[32,1,128]{2,1,0:T(1,128)} %bitcast.3), custom_call_target="tpu_custom_call" | custom-call | tf_op jit(solution)/shard_map/columns/pallas_call | solution.py:505
  63.6 2.6 %unpack.1 = (f32[32,2,128,128]{3,2,1,0:T(8,128)}, f32[32,128]{1,0:T(8,128)}, f32[2]{0:T(128)}) custom-call(s32[8,1,128]{2,1,0:T(1,128)S(1)} %get-tuple-element.10.tab, bf16[4,8,2,128,128]{4,3,2,1,0:T(8,128)(2,1)S(1)} %get-tuple-element.11.fin_ref, f32[4,8,128]{2,1,0:T(8,128)S(1)} %get-tuple-element.12.tails_ref, f32[1,128]{1,0:T(1,128)S(1)} %get-tuple-element.13.whole_ref), custom_call_target="tpu_custom_call" | custom-call | tf_op jit(solution)/shard_map/unpack/pallas_call | solution.py:544

commit v6 on v5

--- a/solution.py
+++ b/solution.py
@@ -326,7 +326,7 @@
         learn(distant + beside)
         send(distant, [0], inner_turns)
         send(beside, range(samp), near_turns)
-        send(across, [1], inner_turns)
+        send_by_core((1,), inner_turns)
         send_by_core((2, 3), inner_turns)
 
     @pl.when(inner == 0)

time: 66.6 us -> 66.6 us (level)
  no operation moved by 1% of the time
where the time goes in v6:
time: 66.6 us; the launch traced here: 66.3 us
  Pallas kernels  65.6 us (98%)
    pallas_call x1, Pallas kernels, column_body(): pl.pallas_call(functools.partial(main_kernel, samp, var), out_shape=(jax....  63 us
    pallas_call x1, Pallas kernels, column_body(): pl.pallas_call(functools.partial(unpack_kernel, samp, var, float(cols * w...  2.65 us

profile of v6, /device:TPU:0, one launch (start us, length us, event | category | flops | bytes accessed | tf_op | source)
XLA Modules:
  0.0 66.3 jit_solution(9254738917861455829)
XLA Ops:
  0.6 63.0 %columns.1 = (bf16[4,8,2,128,128]{4,3,2,1,0:T(8,128)(2,1)S(1)}, f32[4,8,128]{2,1,0:T(8,128)S(1)}, f32[1,128]{1,0:T(1,128)S(1)}, s32[8,1,128]{2,1,0:T(1,128)S(1)}) custom-call(s32[2,32]{1,0:T(2,128)} %bitcast.4, bf16[256,4096]{1,0:T(8,128)(2,1)} %x_hbm.1, f32[32,2,128,128]{3,2,1,0:T(8,128)} %blk_hbm.1, f32[32,1,128]{2,1,0:T(1,128)} %bitcast.3), custom_call_target="tpu_custom_call" | custom-call | tf_op jit(solution)/shard_map/columns/pallas_call | solution.py:505
  63.6 2.6 %unpack.1 = (f32[32,2,128,128]{3,2,1,0:T(8,128)}, f32[32,128]{1,0:T(8,128)}, f32[2]{0:T(128)}) custom-call(s32[8,1,128]{2,1,0:T(1,128)S(1)} %get-tuple-element.10.tab, bf16[4,8,2,128,128]{4,3,2,1,0:T(8,128)(2,1)S(1)} %get-tuple-element.11.fin_ref, f32[4,8,128]{2,1,0:T(8,128)S(1)} %get-tuple-element.12.tails_ref, f32[1,128]{1,0:T(1,128)S(1)} %get-tuple-element.13.whole_ref), custom_call_target="tpu_custom_call" | custom-call | tf_op jit(solution)/shard_map/unpack/pallas_call | solution.py:544
